TPU v7x, 512 devices: a whole 4x8x8 slice. The times are simulated.
512 devices in a mesh: row: 8 (over y), col: 64 (over x, z, core).
Axes of the slice: x: 4, y: 8, z: 8, core: 2. Of those that a mesh axis runs over, the one named last changes fastest.
Arguments:
- phase_codes: int32 [256, 32768], P('row', 'col'), may hold values from 0 to 4095
- aperture: int32 [256, 32768], P('row', 'col'), may hold values from 0 to 1
- tile_offsets: int32 [16, 64], P('row', 'col'), may hold values from 0 to 4095
Outputs:
- psf_field: float32 [2, 256, 131072], P(None, 'row', 'col')
All inputs are finite; a program needn't handle non-finite values.
Results may differ from a plain program's by a relative error of at most 0.00013.
Values sent between devices are 32-bit elements; how exact they have to be, the bound alone decides.
A program may use at most 64 MiB of HBM per device.

v0:
```python
import math

import jax
import jax.numpy as jnp
from jax import lax
from jax.sharding import PartitionSpec as P

LEVELS = 4096
TILE_R = 16
TILE_C = 512


def from_partner(value, axis, distance):
    mask = 2**distance
    pairs = [(source, source ^ mask) for source in range(lax.axis_size(axis))]
    return lax.ppermute(value, axis, pairs)


def angle_table(first_idx, second_idx, modulus):
    product = first_idx[:, None] * second_idx[None, :] % modulus
    return product.astype(jnp.float32) * (2.0 * math.pi / modulus)


def per_device(phase_codes, aperture, tile_offsets):
    n_col = lax.axis_size("col")
    n_row = lax.axis_size("row")
    bit_count = n_col.bit_length() - 1
    col_index = lax.axis_index("col")
    row_index = lax.axis_index("row")
    row_dev, pupil_dev = phase_codes.shape
    tile_rows, tile_cols = tile_offsets.shape
    running = jnp.cumsum(tile_offsets, axis=0) % LEVELS
    totals = running[-1, :]
    every_total = lax.all_gather(totals[None, :], "row", axis=0, tiled=True)
    earlier = jnp.arange(every_total.shape[0], dtype=jnp.int32) < row_index
    before = jnp.sum(jnp.where(earlier[:, None], every_total, 0), axis=0) % LEVELS
    piston = (before[None, :] + running) % LEVELS
    codes = phase_codes.reshape(tile_rows, TILE_R, tile_cols, TILE_C) + piston[:, None, :, None]
    codes = (codes % LEVELS).reshape(row_dev, pupil_dev)
    theta = codes.astype(jnp.float32) * (2.0 * math.pi / LEVELS)
    amplitude = aperture.astype(jnp.float32)
    field = jnp.stack([amplitude * jnp.cos(theta), amplitude * jnp.sin(theta)])
    open_count = lax.psum(jnp.sum(aperture), ("row", "col"))
    scale = jnp.sqrt(jnp.float32(row_dev * n_row) / open_count.astype(jnp.float32))
    fold = pupil_dev // n_col
    arranged = field.reshape((2, row_dev, fold) + (2,) * bit_count)
    axis_order = (0, 1) + tuple(range(bit_count + 2, 2, -1)) + (2,)
    arranged = jnp.transpose(arranged, axis_order).reshape(2, row_dev, n_col, fold)
    received = lax.all_to_all(arranged, "col", split_axis=2, concat_axis=3, tiled=True)
    freq_len = fold * n_col
    pad_len = 4 * freq_len
    pupil_part = received.reshape(2, row_dev, freq_len)
    idx_f = jnp.arange(freq_len, dtype=jnp.int32)
    pre_angle = angle_table(jnp.arange(4, dtype=jnp.int32), idx_f, pad_len)
    pre_cos = jnp.cos(pre_angle)[None, :, :]
    pre_sin = jnp.sin(pre_angle)[None, :, :]
    real_in = pupil_part[0][:, None, :]
    imag_in = pupil_part[1][:, None, :]
    shifted = jnp.stack(
        [real_in * pre_cos + imag_in * pre_sin, imag_in * pre_cos - real_in * pre_sin]
    )
    main_angle = angle_table(idx_f, idx_f, freq_len)
    with_cos = jnp.einsum(
        "xraf,sf->xras", shifted, jnp.cos(main_angle), precision=lax.Precision.HIGHEST
    )
    with_sin = jnp.einsum(
        "xraf,sf->xras", shifted, jnp.sin(main_angle), precision=lax.Precision.HIGHEST
    )
    spec_re = jnp.transpose(with_cos[0] + with_sin[1], (0, 2, 1)).reshape(row_dev, pad_len)
    spec_im = jnp.transpose(with_cos[1] - with_sin[0], (0, 2, 1)).reshape(row_dev, pad_len)
    own_residue = jnp.zeros((), jnp.int32)
    for place_bit in range(bit_count):
        own_residue = own_residue + col_index // 2**place_bit % 2 * 2 ** (bit_count - 1 - place_bit)
    total_len = pad_len * n_col
    twist = own_residue * jnp.arange(pad_len, dtype=jnp.int32) % total_len
    twist_angle = twist.astype(jnp.float32) * (2.0 * math.pi / total_len)
    tw_cos = jnp.cos(twist_angle)[None, :]
    tw_sin = jnp.sin(twist_angle)[None, :]
    spectrum = jnp.stack([spec_re * tw_cos + spec_im * tw_sin, spec_im * tw_cos - spec_re * tw_sin])
    for section_bit in range(bit_count):
        half_size = 2**section_bit
        partner = from_partner(spectrum, "col", section_bit)
        upper_half = col_index // half_size % 2 == 1
        within = (col_index % half_size).astype(jnp.float32)
        cos_part = jnp.cos(math.pi * within / half_size)
        sin_part = -jnp.sin(math.pi * within / half_size)
        first_term = jnp.where(upper_half, partner, spectrum)
        second_term = jnp.where(upper_half, spectrum, partner)
        rotated_re = cos_part * second_term[0] - sin_part * second_term[1]
        rotated_im = cos_part * second_term[1] + sin_part * second_term[0]
        sign_term = jnp.where(upper_half, -1.0, 1.0).astype(jnp.float32)
        spectrum = jnp.stack(
            [first_term[0] + sign_term * rotated_re, first_term[1] + sign_term * rotated_im]
        )
    return spectrum * scale


def solution(mesh):
    placed = (P("row", "col"), P("row", "col"), P("row", "col"))
    return jax.shard_map(
        per_device, mesh=mesh, in_specs=placed, out_specs=P(None, "row", "col"), check_vma=False
    )
```

profile of v0, /device:TPU:1, one launch (start us, length us, event | category | flops | bytes accessed | tf_op | source)
XLA Modules:
  0.0 256.3 jit_solution(10987014880057656648)
XLA Ops:
  0.0 0.7 copy-done.1
  0.7 0.2 reduce_window_sum.13
  0.8 0.6 slice.108
  1.5 1.3 dynamic-slice
  2.8 1.3 bitcast_dynamic-update-slice_fusion
  4.1 12.0 %all-reduce = s32[8]{0:T(128)S(1)} all-reduce(s32[8]{0:T(128)S(1)} %bitcast_dynamic-update-slice_fusion), channel_id=1, replica_groups=mesh['row'=8,'col'=64] {'row'}, use_global_device_ids=true, to_apply=%add | all-reduce | flops 8 | bytes 64
  16.1 0.6 fusion.32
  18.7 0.1 add.291
  18.8 1.2 cosine_multiply_fusion
  20.1 0.1 copy.22
  20.2 0.1 copy.23
  20.3 0.4 maximum_bitcast_fusion
  20.7 0.3 copy.36
  21.0 0.9 reshape.360
  21.9 17.1 %all-to-all-start = ((f32[64,1,512]{2,1,0:T(1,128)}), f32[64,1,512]{2,1,0:T(1,128)S(1)}, u32[]{:S(2)}, u32[]{:S(2)}) async-start(f32[64,1,512]{2,1,0:T(1,128)} %reshape.360), calls=%async_computation | async-start | bytes 262144 | tf_op jit(solution)/shard_map/all_to_all | solution.py:49
  39.1 0.1 fusion.30
  39.3 9.9 %all-to-all-done = f32[64,1,512]{2,1,0:T(1,128)S(1)} async-done(((f32[64,1,512]{2,1,0:T(1,128)}), f32[64,1,512]{2,1,0:T(1,128)S(1)}, u32[]{:S(2)}, u32[]{:S(2)}) %all-to-all-start) | async-done | bytes 131104 | tf_op jit(solution)/shard_map/all_to_all | solution.py:49
  49.1 0.5 broadcast.484
  49.7 0.9 reduce.1
  50.6 0.2 reshape.361
  50.8 0.1 copy.26
  50.9 0.1 copy.27
  51.1 4.9 %fusion.5 = f32[2,32,4,512]{3,1,2,0:T(8,128)S(1)} fusion(f32[1,32,4,512]{3,1,2,0:T(8,128)S(1)} %get-tuple-element.36, f32[1,32,4,512]{3,1,2,0:T(8,128)S(1)} %get-tuple-element.35), kind=kOutput, calls=%fused_computation.8 | convolution fusion | flops 809107456 | bytes 1048576 | tf_op jit(solution)/shard_map/xraf,sf->xras/dot_general | solution.py:63
  56.0 4.9 %fusion.3 = f32[2,32,4,512]{3,1,2,0:T(8,128)S(1)} fusion(f32[1,32,4,512]{3,1,2,0:T(8,128)S(1)} %get-tuple-element.36, f32[1,32,4,512]{3,1,2,0:T(8,128)S(1)} %get-tuple-element.35), kind=kOutput, calls=%fused_computation.6 | convolution fusion | flops 809107456 | bytes 1048576 | tf_op jit(solution)/shard_map/xraf,sf->xras/dot_general | solution.py:66
  61.0 0.4 copy.28
  61.4 0.3 copy.29
  61.7 0.4 copy.30
  62.1 0.5 copy.31
  62.8 2.3 collective-permute-start
  65.1 1.5 collective-permute-done
  66.8 3.0 %collective-permute-start.1 = (f32[2,32,2048]{2,1,0:T(8,128)S(1)}, f32[2,32,2048]{2,1,0:T(8,128)S(1)}, u32[]{:S(2)}, u32[]{:S(2)}) collective-permute-start(f32[2,32,2048]{2,1,0:T(8,128)S(1)} %pad_maximum_fusion.2), channel_id=1, source_target_pairs={{0,2},{1,3},{2,0},{3,1},{4,6},{5,7},{6,4},{7,5},{8,10},{9,11},{10,... | collective-permute-start | bytes 1572872 | tf_op jit(solution)/shard_map/ppermute | solution.py:16
  69.9 11.9 %collective-permute-done.1 = f32[2,32,2048]{2,1,0:T(8,128)S(1)} collective-permute-done((f32[2,32,2048]{2,1,0:T(8,128)S(1)}, f32[2,32,2048]{2,1,0:T(8,128)S(1)}, u32[]{:S(2)}, u32[]{:S(2)}) %collective-permute-start.1) | collective-permute-done | bytes 524320 | tf_op jit(solution)/shard_map/ppermute | solution.py:16
  81.9 0.1 slice_add_fusion.9
  82.1 3.2 %collective-permute-start.2 = (f32[2,32,2048]{2,1,0:T(8,128)S(1)}, f32[2,32,2048]{2,1,0:T(8,128)S(1)}, u32[]{:S(2)}, u32[]{:S(2)}) collective-permute-start(f32[2,32,2048]{2,1,0:T(8,128)S(1)} %pad_maximum_fusion.3), channel_id=1, source_target_pairs={{0,4},{1,5},{2,6},{3,7},{4,0},{5,1},{6,2},{7,3},{8,12},{9,13},{10,... | collective-permute-start | bytes 1572872 | tf_op jit(solution)/shard_map/ppermute | solution.py:16
  85.4 23.8 %collective-permute-done.2 = f32[2,32,2048]{2,1,0:T(8,128)S(1)} collective-permute-done((f32[2,32,2048]{2,1,0:T(8,128)S(1)}, f32[2,32,2048]{2,1,0:T(8,128)S(1)}, u32[]{:S(2)}, u32[]{:S(2)}) %collective-permute-start.2) | collective-permute-done | bytes 524320 | tf_op jit(solution)/shard_map/ppermute | solution.py:16
  109.3 0.1 slice_add_fusion.7
  109.4 3.5 %collective-permute-start.3 = (f32[2,32,2048]{2,1,0:T(8,128)S(1)}, f32[2,32,2048]{2,1,0:T(8,128)S(1)}, u32[]{:S(2)}, u32[]{:S(2)}) collective-permute-start(f32[2,32,2048]{2,1,0:T(8,128)S(1)} %pad_maximum_fusion.4), channel_id=1, source_target_pairs={{0,8},{1,9},{2,10},{3,11},{4,12},{5,13},{6,14},{7,15},{8,0},{9,1},... | collective-permute-start | bytes 1572872 | tf_op jit(solution)/shard_map/ppermute | solution.py:16
  113.1 25.5 %collective-permute-done.3 = f32[2,32,2048]{2,1,0:T(8,128)S(1)} collective-permute-done((f32[2,32,2048]{2,1,0:T(8,128)S(1)}, f32[2,32,2048]{2,1,0:T(8,128)S(1)}, u32[]{:S(2)}, u32[]{:S(2)}) %collective-permute-start.3) | collective-permute-done | bytes 524320 | tf_op jit(solution)/shard_map/ppermute | solution.py:16
  138.8 0.1 slice_add_fusion.5
  138.9 2.6 %collective-permute-start.4 = (f32[2,32,2048]{2,1,0:T(8,128)S(1)}, f32[2,32,2048]{2,1,0:T(8,128)S(1)}, u32[]{:S(2)}, u32[]{:S(2)}) collective-permute-start(f32[2,32,2048]{2,1,0:T(8,128)S(1)} %pad_maximum_fusion.5), channel_id=1, source_target_pairs={{0,16},{1,17},{2,18},{3,19},{4,20},{5,21},{6,22},{7,23},{8,24},{9,... | collective-permute-start | bytes 1572872 | tf_op jit(solution)/shard_map/ppermute | solution.py:16
  141.7 11.9 %collective-permute-done.4 = f32[2,32,2048]{2,1,0:T(8,128)S(1)} collective-permute-done((f32[2,32,2048]{2,1,0:T(8,128)S(1)}, f32[2,32,2048]{2,1,0:T(8,128)S(1)}, u32[]{:S(2)}, u32[]{:S(2)}) %collective-permute-start.4) | collective-permute-done | bytes 524320 | tf_op jit(solution)/shard_map/ppermute | solution.py:16
  153.7 0.1 slice_add_fusion.3
  153.9 1.9 collective-permute-start.5
  155.8 0.6 reduce_sum.22
  156.5 97.9 %psum.7 = s32[]{:T(128)} all-reduce(s32[]{:T(128)} %reduce_sum.22), channel_id=1, replica_groups=mesh['row'=8,'col'=64] {'row','col'}, use_global_device_ids=true, to_apply=%region_3.4 | all-reduce | flops 1 | bytes 8 | tf_op jit(solution)/shard_map/psum | solution.py:43
  255.3 0.1 broadcast_select_fusion.10
  255.4 0.1 slice_add_fusion.1
  255.5 0.8 maximum_multiply_fusion
  (25 shorter events, 1.1 us)
Async XLA Ops:
  0.0 0.7 copy-start.1
  21.9 27.2 %all-to-all-start = ((f32[64,1,512]{2,1,0:T(1,128)}), f32[64,1,512]{2,1,0:T(1,128)S(1)}, u32[]{:S(2)}, u32[]{:S(2)}) async-start(f32[64,1,512]{2,1,0:T(1,128)} %reshape.360), calls=%async_computation | async-start | bytes 262144 | tf_op jit(solution)/shard_map/all_to_all | solution.py:49
  62.8 3.8 %collective-permute-start = (f32[2,32,2048]{2,1,0:T(8,128)S(1)}, f32[2,32,2048]{2,1,0:T(8,128)S(1)}, u32[]{:S(2)}, u32[]{:S(2)}) collective-permute-start(f32[2,32,2048]{2,1,0:T(8,128)S(1)} %pad_maximum_fusion.1), channel_id=1, source_target_pairs={{0,1},{1,0},{2,3},{3,2},{4,5},{5,4},{6,7},{7,6},{8,9},{9,8},{10,11... | collective-permute-start | bytes 1572872 | tf_op jit(solution)/shard_map/ppermute | solution.py:16
  66.8 15.0 %collective-permute-start.1 = (f32[2,32,2048]{2,1,0:T(8,128)S(1)}, f32[2,32,2048]{2,1,0:T(8,128)S(1)}, u32[]{:S(2)}, u32[]{:S(2)}) collective-permute-start(f32[2,32,2048]{2,1,0:T(8,128)S(1)} %pad_maximum_fusion.2), channel_id=1, source_target_pairs={{0,2},{1,3},{2,0},{3,1},{4,6},{5,7},{6,4},{7,5},{8,10},{9,11},{10,... | collective-permute-start | bytes 1572872 | tf_op jit(solution)/shard_map/ppermute | solution.py:16
  82.1 27.1 %collective-permute-start.2 = (f32[2,32,2048]{2,1,0:T(8,128)S(1)}, f32[2,32,2048]{2,1,0:T(8,128)S(1)}, u32[]{:S(2)}, u32[]{:S(2)}) collective-permute-start(f32[2,32,2048]{2,1,0:T(8,128)S(1)} %pad_maximum_fusion.3), channel_id=1, source_target_pairs={{0,4},{1,5},{2,6},{3,7},{4,0},{5,1},{6,2},{7,3},{8,12},{9,13},{10,... | collective-permute-start | bytes 1572872 | tf_op jit(solution)/shard_map/ppermute | solution.py:16
  109.4 29.3 %collective-permute-start.3 = (f32[2,32,2048]{2,1,0:T(8,128)S(1)}, f32[2,32,2048]{2,1,0:T(8,128)S(1)}, u32[]{:S(2)}, u32[]{:S(2)}) collective-permute-start(f32[2,32,2048]{2,1,0:T(8,128)S(1)} %pad_maximum_fusion.4), channel_id=1, source_target_pairs={{0,8},{1,9},{2,10},{3,11},{4,12},{5,13},{6,14},{7,15},{8,0},{9,1},... | collective-permute-start | bytes 1572872 | tf_op jit(solution)/shard_map/ppermute | solution.py:16
  138.9 14.7 %collective-permute-start.4 = (f32[2,32,2048]{2,1,0:T(8,128)S(1)}, f32[2,32,2048]{2,1,0:T(8,128)S(1)}, u32[]{:S(2)}, u32[]{:S(2)}) collective-permute-start(f32[2,32,2048]{2,1,0:T(8,128)S(1)} %pad_maximum_fusion.5), channel_id=1, source_target_pairs={{0,16},{1,17},{2,18},{3,19},{4,20},{5,21},{6,22},{7,23},{8,24},{9,... | collective-permute-start | bytes 1572872 | tf_op jit(solution)/shard_map/ppermute | solution.py:16
  153.8 2.0 copy-start
  153.9 101.4 %collective-permute-start.5 = (f32[2,32,2048]{2,1,0:T(8,128)S(1)}, f32[2,32,2048]{2,1,0:T(8,128)S(1)}, u32[]{:S(2)}, u32[]{:S(2)}) collective-permute-start(f32[2,32,2048]{2,1,0:T(8,128)S(1)} %pad_maximum_fusion.6), channel_id=1, source_target_pairs={{0,32},{1,33},{2,34},{3,35},{4,36},{5,37},{6,38},{7,39},{8,40},{9,... | collective-permute-start | bytes 1572872 | tf_op jit(solution)/shard_map/ppermute | solution.py:16
where the time goes:
time: 257 us; the launch traced here: 256 us
  blocking collectives  110 us (43%)
  waiting for transfers between devices  84.4 us (33%)
  starting transfers between devices  33.6 us (13%)
  matrix products  9.81 us (4%)
  local copies, waits for them, and re-layouts  8.01 us (3%)
  other arithmetic  6.49 us (3%)
  between operations  4.04 us (2%)
    psum x1, blocking collectives, per_device(): open_count = lax.psum(jnp.sum(aperture), ('row', 'col'))  97.9 us
    ppermute x6, waiting for transfers between devices, from_partner(): return lax.ppermute(value, axis, pairs)  74.6 us
    all_to_all x1, starting transfers between devices, per_device(): lax.all_to_all(arranged, 'col', split_axis=2, concat_axis=3, tiled=True)  17.1 us
    ppermute x6, starting transfers between devices, from_partner(): return lax.ppermute(value, axis, pairs)  16.5 us
    unnamed x1, blocking collectives  12 us
    all_to_all x1, waiting for transfers between devices, per_device(): lax.all_to_all(arranged, 'col', split_axis=2, concat_axis=3, tiled=True)  9.86 us
  transfers between devices with their start and end apart: 7, of which 6 were waited for; matrix products, arithmetic and copies ran while one was open for 0% of the time, Pallas kernels for 0%

commit v1 on v0

v1 whole, which is shorter than its diff:
```python
import functools
import math

import jax
import jax.numpy as jnp
from jax import lax
from jax.experimental import pallas as pl
from jax.experimental.pallas import tpu as pltpu
from jax.sharding import PartitionSpec as P

MESH = pl.DeviceIdType.MESH
F32, I32, BF16 = jnp.float32, jnp.int32, jnp.bfloat16

NY, NX, NZ, NCORE = 8, 4, 8, 2
NB = NX * NCORE
ROWS = 32
HALF = 16
GROUPS = 2
GROWS = HALF // GROUPS
CHUNKS = 4
CROWS = HALF // CHUNKS


def cos_sin(index, bits):
    size = 1 << bits
    index = index & (size - 1)
    quadrant = (index + (size >> 3)) >> (bits - 2)
    rest = index - (quadrant << (bits - 2))
    x = rest.astype(F32) * F32(2.0 * math.pi / size)
    y = x * x
    s = x * (1.0 + y * (-1.0 / 6 + y * (1.0 / 120 + y * (-1.0 / 5040 + y * (1.0 / 362880)))))
    c = 1.0 + y * (-0.5 + y * (1.0 / 24 + y * (-1.0 / 720 + y * (1.0 / 40320))))
    quadrant = quadrant & 3
    swap = (quadrant & 1) == 1
    cos = jnp.where(swap, s, c)
    sin = jnp.where(swap, c, s)
    cos = jnp.where((quadrant == 1) | (quadrant == 2), -cos, cos)
    sin = jnp.where(quadrant >= 2, -sin, sin)
    return cos, sin


def halves(value):
    high = value.astype(BF16)
    return high, (value - high.astype(F32)).astype(BF16)


def iota(shape, axis):
    return lax.broadcasted_iota(I32, shape, axis)


def rotation(cos, sin, part_out, part_in):
    cross = jnp.where(part_out == 0, sin, -sin)
    return jnp.where(part_out == part_in, cos, cross)


def kernel(codes, aperture, offsets, out, yslots, xslots, zslots, p1s, p1r, gathered,
           tcos, tsin, wmat, emat, zsend, zrecv, fsend,
           ysend, yrecv, axsend, axrecv, azsend, azrecv, p1send, p1recv,
           p2send, p2recv, asend, arecv, bsend, brecv):
    y = lax.axis_index("row")
    col = lax.axis_index("col")
    core = col % NCORE
    z = (col // NCORE) % NZ
    x = col // (NCORE * NZ)
    me = x * NCORE + core

    def at_y(k):
        return (k, col)

    def at_b(k):
        return (y, ((k // NCORE) * NZ + z) * NCORE + k % NCORE)

    def at_z(k):
        return (y, (x * NZ + k) * NCORE + core)

    def remote(src, dst, ss, rs, where):
        return pltpu.make_async_remote_copy(
            src_ref=src, dst_ref=dst, send_sem=ss, recv_sem=rs,
            device_id=where, device_id_type=MESH)

    barrier = pltpu.get_barrier_semaphore()

    @pl.loop(1, 8)
    def _(k):
        for where in (at_y((y + k) % NY), at_b((me + k) % NB), at_z((z + k) % NZ)):
            pl.semaphore_signal(barrier, inc=1, device_id=where, device_id_type=MESH)

    off0, off1 = offsets[0, 0], offsets[1, 0]
    opened = aperture[...]
    per_lane = jnp.sum(opened, axis=0, keepdims=True)
    count = sum(per_lane[:, j * 128:(j + 1) * 128] for j in range(4))
    yslots[y, 0:1, :] = jnp.full((1, 128), off0 + off1, I32)
    yslots[y, 1:2, :] = count

    row = iota((ROWS, 512), 0)
    code = codes[...] + jnp.where(row < 16, off0, off0 + off1)
    code = code & 4095
    marked = jnp.concatenate([(code >> 6) + 64 * opened, code & 63], axis=0)
    i, j = iota((512, 512), 0), iota((512, 512), 1)
    pick = jnp.where(i == 4 * (j & 127) + (j >> 7), 1.0, 0.0).astype(BF16)
    moved = jnp.dot(marked.astype(F32).astype(BF16), pick, preferred_element_type=F32)
    moved = moved.astype(I32)
    high, low = moved[:ROWS], moved[ROWS:]
    amplitude = (high >> 6).astype(F32)
    cos, sin = cos_sin(((high & 63) << 6) + low, 12)
    field = (amplitude * cos, amplitude * sin)
    for b in range(NB):
        bx, bc = b // NCORE, b % NCORE
        for part in range(2):
            p1s[b * 32 + part * 16:b * 32 + part * 16 + 16, :] = (
                field[part][bc * HALF:(bc + 1) * HALF, bx * 128:(bx + 1) * 128])

    pl.semaphore_wait(barrier, 21)

    def y_copy(peer):
        return remote(yslots.at[y], yslots.at[y], ysend.at[peer], yrecv.at[y], at_y(peer))

    def p1_copy(peer):
        return remote(p1s.at[pl.ds(peer * 32, 32), :], p1r.at[pl.ds(me * 32, 32), :],
                      p1send.at[peer], p1recv.at[me], at_b(peer))

    @pl.loop(1, 8)
    def _(k):
        y_copy((y + k) % NY).start()
        p1_copy((me + k) % NB).start()

    p1r[pl.ds(pl.multiple_of(me * 32, 32), 32), :] = p1s[pl.ds(pl.multiple_of(me * 32, 32), 32), :]

    @pl.loop(1, 8)
    def _(k):
        peer = (y + k) % NY
        remote(yslots.at[peer], yslots.at[peer], ysend.at[peer], yrecv.at[peer],
               at_y(peer)).wait_recv()

    before = jnp.zeros((1, 128), I32)
    count = jnp.zeros((1, 128), I32)
    for k in range(NY):
        before = before + jnp.where(k < y, yslots[k, 0:1, :], 0)
        count = count + yslots[k, 1:2, :]
    xslots[me, 0:1, :] = before & 4095
    xslots[me, 1:2, :] = count

    def ax_copy(peer):
        return remote(xslots.at[me], xslots.at[me], axsend.at[peer], axrecv.at[me], at_b(peer))

    @pl.loop(1, 8)
    def _(k):
        ax_copy((me + k) % NB).start()

    @pl.loop(1, 8)
    def _(k):
        peer = (me + k) % NB
        remote(p1s.at[pl.ds(peer * 32, 32), :], p1r.at[pl.ds(peer * 32, 32), :],
               p1send.at[peer], p1recv.at[peer], at_b(peer)).wait_recv()

    for n in range(HALF):
        for part in range(2):
            gathered[z, n, part * 8:(part + 1) * 8, :] = (
                p1r[pl.ds(part * 16 + n, NB, stride=32), :])

    right, left = (z + 1) % NZ, (z + NZ - 1) % NZ

    def ring(block, chunk, way, step):
        part = gathered.at[block, pl.ds(chunk * CROWS, CROWS)]
        return remote(part, part, p2send.at[way, step, chunk], p2recv.at[block, chunk],
                      at_z(right if way == 0 else left))

    def arrived(block, chunk):
        part = gathered.at[block, pl.ds(chunk * CROWS, CROWS)]
        remote(part, part, p2send.at[0, 0, chunk], p2recv.at[block, chunk],
               at_z(left)).wait_recv()

    for chunk in range(CHUNKS):
        ring(z, chunk, 0, 0).start()
        ring(z, chunk, 1, 0).start()

    @pl.loop(1, 8)
    def _(k):
        peer = (me + k) % NB
        remote(xslots.at[peer], xslots.at[peer], axsend.at[peer], axrecv.at[peer],
               at_b(peer)).wait_recv()
    zslots[z, 0:8, :] = xslots[:, 0, :]
    zslots[z, 8:16, :] = xslots[:, 1, :]

    def az_copy(peer):
        return remote(zslots.at[z], zslots.at[z], azsend.at[peer], azrecv.at[z], at_z(peer))

    @pl.loop(1, 8)
    def _(k):
        az_copy((z + k) % NZ).start()

    shape = (512, 128)
    i, j = iota(shape, 0), iota(shape, 1)
    source = j & 7
    a = ((source >> 1) * NZ + ((j >> 3) & 7)) * NCORE + (source & 1)
    cos, sin = cos_sin(a * (i & 255), 8)
    w_high, w_low = halves(rotation(cos, sin, i >> 8, j >> 6))
    wmat[:, 0:128] = w_high
    wmat[:, 128:256] = w_high
    wmat[:, 256:384] = w_low
    shape = (256, 128)
    cos, sin = cos_sin((4 * iota(shape, 1) + x) * iota(shape, 0), 17)
    tcos[...] = cos
    tsin[...] = sin
    shape = (32, 256)
    i, j = iota(shape, 0), iota(shape, 1)
    q = 2 * (i >> 3) + ((i >> 1) & 1)
    d_low = NCORE * z + ((i >> 2) & 1)
    cos, sin = cos_sin((4 * (j & 127) + x) * (8 * d_low + q), 9)
    e_high, e_low = halves(rotation(cos, sin, i & 1, j >> 7))
    emat[0:32, :] = e_high
    emat[32:64, :] = e_low

    for step in range(1, 4):
        for chunk in range(CHUNKS):
            for way in range(2):
                block = (z + NZ - step) % NZ if way == 0 else (z + step) % NZ
                arrived(block, chunk)
                if step < 3 or (chunk < CHUNKS // 2) == (way == 0):
                    ring(block, chunk, way, step).start()

    @pl.loop(1, 8)
    def _(k):
        peer = (z + k) % NZ
        remote(zslots.at[peer], zslots.at[peer], azsend.at[peer], azrecv.at[peer],
               at_z(peer)).wait_recv()
    pcos, psin = cos_sin(zslots[:, 0:8, :], 12)
    total = jnp.sum(zslots[:, 8:16, :], axis=0)
    total = jnp.sum(jnp.sum(total.astype(F32), axis=0, keepdims=True), axis=1, keepdims=True)
    scale = jnp.sqrt(F32(ROWS * NY) / total)

    for chunk in range(CHUNKS):
        arrived((z + 4) % NZ, chunk)

    nt = (((1,), (1,)), ((), ()))

    def a_copy(g, peer):
        return remote(zsend.at[g, :, pl.ds(peer * 8 * GROWS, 8 * GROWS), :], zrecv.at[x, g],
                      asend.at[g, peer], arecv.at[g, x], at_b(peer * NCORE + core))

    for g in range(GROUPS):
        @pl.loop(0, GROWS // 2)
        def _(pair, g=g):
            columns = []
            for n in range(2):
                block = gathered[:, g * GROWS + pair * 2 + n]
                re, im = block[:, 0:8, :], block[:, 8:16, :]
                columns.append(jnp.concatenate(
                    [(re * pcos - im * psin).reshape(64, 128),
                     (re * psin + im * pcos).reshape(64, 128)], axis=0))
            high, low = halves(jnp.concatenate(columns, axis=1))
            spec = jnp.dot(wmat[...], jnp.concatenate([high, low, high], axis=0),
                           preferred_element_type=F32)
            for n in range(2):
                re = spec[0:256, n * 128:(n + 1) * 128]
                im = spec[256:512, n * 128:(n + 1) * 128]
                c, s = tcos[...], tsin[...]
                turned = jnp.concatenate([re * c + im * s, im * c - re * s], axis=1)
                high, low = halves(turned)
                first = lax.dot_general(emat[...], high, nt, preferred_element_type=F32)
                second = lax.dot_general(emat[0:32, :], low, nt, preferred_element_type=F32)
                result = first[0:32] + first[32:64] + second
                for h in range(2):
                    zsend[g, h, pl.ds(pair * 2 + n, 32, stride=GROWS), :] = (
                        result[:, h * 128:(h + 1) * 128])

        for k in range(1, NX):
            a_copy(g, (x + k) % NX).start()
        zrecv[x, g] = zsend[g, :, pl.ds(pl.multiple_of(x * 8 * GROWS, 8 * GROWS), 8 * GROWS), :]

    def b_copy(g, peer):
        return remote(fsend.at[g, peer],
                      out.at[:, pl.ds(core * HALF + g * GROWS, GROWS), pl.ds(pl.multiple_of(x * 512, 512), 512)],
                      bsend.at[g, peer], brecv.at[g, me], at_b(peer))

    for g in range(GROUPS):
        for k in range(1, NX):
            peer = (x + k) % NX
            remote(zrecv.at[peer, g], zrecv.at[peer, g], asend.at[g, peer], arecv.at[g, peer],
                   at_b(peer * NCORE + core)).wait_recv()
        for dc in range(2):
            for qh in range(4):
                ql, h = qh // 2, qh % 2
                part = []
                for p in range(2):
                    start = ((dc * 2 + ql) * 2 + p) * GROWS
                    part.append([zrecv[b, g, h, start:start + GROWS, :] * scale for b in range(NX)])
                (r0, r1, r2, r3), (i0, i1, i2, i3) = part
                ar, ai, br, bi = r0 + r2, i0 + i2, r1 + r3, i1 + i3
                dr, di, er, ei = r0 - r2, i0 - i2, r1 - r3, i1 - i3
                results = ((ar + br, ai + bi), (dr + ei, di - er), (ar - br, ai - bi), (dr - ei, di + er))
                for dx in range(NX):
                    for p in range(2):
                        fsend[g, dx * NCORE + dc, p, :, qh * 128:(qh + 1) * 128] = results[dx][p]

        @pl.loop(1, 8)
        def _(k, g=g):
            b_copy(g, (me + k) % NB).start()
        out[:, pl.ds(pl.multiple_of(core * HALF + g * GROWS, GROWS), GROWS),
            pl.ds(pl.multiple_of(x * 512, 512), 512)] = fsend[g, me]

    for g in range(GROUPS):
        @pl.loop(1, 8)
        def _(k, g=g):
            peer = (me + k) % NB
            landing = out.at[:, pl.ds((peer % NCORE) * HALF + g * GROWS, GROWS),
                             pl.ds(pl.multiple_of((peer // NCORE) * 512, 512), 512)]
            remote(landing, landing, bsend.at[g, peer], brecv.at[g, peer], at_b(peer)).wait_recv()

    @pl.loop(1, 8)
    def _(k):
        y_copy((y + k) % NY).wait_send()
        p1_copy((me + k) % NB).wait_send()
        ax_copy((me + k) % NB).wait_send()
        az_copy((z + k) % NZ).wait_send()
        for g in range(GROUPS):
            b_copy(g, (me + k) % NB).wait_send()
    for step in range(4):
        for chunk in range(CHUNKS):
            for way in range(2):
                if step < 3 or (chunk < CHUNKS // 2) == (way == 0):
                    block = (z + NZ - step) % NZ if way == 0 else (z + step) % NZ
                    ring(block, chunk, way, step).wait_send()
    for g in range(GROUPS):
        for k in range(1, NX):
            a_copy(g, (x + k) % NX).wait_send()


def per_device(phase_codes, aperture, tile_offsets):
    dma = pltpu.SemaphoreType.DMA
    vmem = pltpu.VMEM
    return pl.pallas_call(
        kernel,
        out_shape=jax.ShapeDtypeStruct((2, ROWS, 2048), F32),
        in_specs=[pl.BlockSpec(memory_space=pltpu.VMEM),
                  pl.BlockSpec(memory_space=pltpu.VMEM),
                  pl.BlockSpec(memory_space=pltpu.SMEM)],
        out_specs=pl.BlockSpec(memory_space=pltpu.VMEM),
        scratch_shapes=[
            vmem((NY, 2, 128), I32), vmem((NB, 2, 128), I32), vmem((NZ, 16, 128), I32),
            vmem((NB * 32, 128), F32), vmem((NB * 32, 128), F32),
            vmem((NZ, HALF, 16, 128), F32),
            vmem((256, 128), F32), vmem((256, 128), F32),
            vmem((512, 384), BF16), vmem((64, 256), BF16),
            vmem((GROUPS, 2, 32 * GROWS, 128), F32),
            vmem((NX, GROUPS, 2, 8 * GROWS, 128), F32),
            vmem((GROUPS, NB, 2, GROWS, 512), F32),
            dma((NY,)), dma((NY,)), dma((NB,)), dma((NB,)), dma((NZ,)), dma((NZ,)),
            dma((NB,)), dma((NB,)),
            dma((2, 4, CHUNKS)), dma((NZ, CHUNKS)),
            dma((GROUPS, NX)), dma((GROUPS, NX)), dma((GROUPS, NB)), dma((GROUPS, NB)),
        ],
        compiler_params=pltpu.CompilerParams(collective_id=0, has_side_effects=True),
    )(phase_codes, aperture, tile_offsets)


def solution(mesh):
    placed = (P("row", "col"), P("row", "col"), P("row", "col"))
    return jax.shard_map(
        per_device, mesh=mesh, in_specs=placed, out_specs=P(None, "row", "col"), check_vma=False
    )
```

time: 257 us -> 60.4 us (0.24)
  blocking collectives: 110 us -> 0 us
  waiting for transfers between devices: 84.4 us -> 0 us
  Pallas kernels: 0 us -> 57 us
  starting transfers between devices: 33.6 us -> 0 us
  matrix products: 9.81 us -> 0 us
  other arithmetic: 6.49 us -> 0 us
  local copies, waits for them, and re-layouts: 8.01 us -> 3.17 us
  between operations: 4.04 us -> 0.01 us
    psum x1 -> x0, blocking collectives: 97.9 us -> none  [per_device(): open_count = lax.psum(jnp.sum(aperture), ('row', 'col'))]
    ppermute x6 -> x0, waiting for transfers between devices: 74.6 us -> none  [from_partner(): return lax.ppermute(value, axis, pairs)]
    pallas_call x0 -> x1, Pallas kernels: none -> 57 us  [per_device(): pl.pallas_call(kernel, out_shape=jax.ShapeDtypeStruct((2, ROWS, 2048), F3...]
    all_to_all x1 -> x0, starting transfers between devices: 17.1 us -> none  [per_device(): lax.all_to_all(arranged, 'col', split_axis=2, concat_axis=3, tiled=True)]
    ppermute x6 -> x0, starting transfers between devices: 16.5 us -> none  [from_partner(): return lax.ppermute(value, axis, pairs)]
    unnamed x1 -> x0, blocking collectives: 12 us -> none
    all_to_all x1 -> x0, waiting for transfers between devices: 9.86 us -> none  [per_device(): lax.all_to_all(arranged, 'col', split_axis=2, concat_axis=3, tiled=True)]
    dot_general x2 -> x0, matrix products: 9.81 us -> none  [the longest x1 4.92 us: per_device(): jnp.einsum('xraf,sf->xras', shifted, jnp.sin(main_angle), precision=lax.P...]
  transfers between devices with their start and end apart: 7 -> 0, of which waited for: 6 -> 0; matrix products, arithmetic and copies ran while one was open for 0% -> 0% of each run, Pallas kernels for 0% -> 0%
where the time goes in v1:
time: 60.4 us; the launch traced here: 60.2 us
  Pallas kernels  57 us (94%)
  local copies, waits for them, and re-layouts  3.17 us (5%)
    pallas_call x1, Pallas kernels, per_device(): pl.pallas_call(kernel, out_shape=jax.ShapeDtypeStruct((2, ROWS, 2048), F3...  57 us
    unnamed x2, local copies, waits for them, and re-layouts  3.17 us

profile of v1, /device:TPU:1, one launch (start us, length us, event | category | flops | bytes accessed | tf_op | source)
XLA Modules:
  0.0 60.2 jit_solution(15234754737962000402)
XLA Ops:
  0.0 1.3 %copy.4.offsets = s32[2,1]{1,0:T(2,128)} copy(s32[2,1]{0,1:T(1,128)} %param.5) | data formatting | bytes 16 | tf_op args[2]
  1.3 57.0 %shard_map.37 = f32[2,32,2048]{2,1,0:T(8,128)} custom-call(s32[32,512]{1,0:T(8,128)} %codes.1, s32[32,512]{1,0:T(8,128)} %aperture.1, s32[2,1]{1,0:T(2,128)} %copy.4.offsets), custom_call_target="tpu_custom_call" | custom-call | tf_op jit(solution)/shard_map/pallas_call | solution.py:332
  58.3 1.9 %copy.6 = f32[2,32,2048]{2,1,0:T(8,128)} copy(f32[2,32,2048]{2,1,0:T(8,128)} %shard_map.37) | data formatting | bytes 1048576

commit v2 on v1

v2 whole, which is shorter than its diff:
```python
import functools
import math

import jax
import jax.numpy as jnp
from jax import lax
from jax.experimental import pallas as pl
from jax.experimental.pallas import tpu as pltpu
from jax.sharding import PartitionSpec as P

MESH = pl.DeviceIdType.MESH
F32, I32, BF16 = jnp.float32, jnp.int32, jnp.bfloat16

NY, NX, NZ, NCORE = 8, 4, 8, 2
NB = NX * NCORE
ROWS = 32
HALF = 16
GROUPS = 4
GROWS = HALF // GROUPS


def cos_sin(index, bits):
    size = 1 << bits
    index = index & (size - 1)
    quadrant = (index + (size >> 3)) >> (bits - 2)
    rest = index - (quadrant << (bits - 2))
    x = rest.astype(F32) * F32(2.0 * math.pi / size)
    y = x * x
    s = x * (1.0 + y * (-1.0 / 6 + y * (1.0 / 120 + y * (-1.0 / 5040 + y * (1.0 / 362880)))))
    c = 1.0 + y * (-0.5 + y * (1.0 / 24 + y * (-1.0 / 720 + y * (1.0 / 40320))))
    quadrant = quadrant & 3
    swap = (quadrant & 1) == 1
    cos = jnp.where(swap, s, c)
    sin = jnp.where(swap, c, s)
    cos = jnp.where((quadrant == 1) | (quadrant == 2), -cos, cos)
    sin = jnp.where(quadrant >= 2, -sin, sin)
    return cos, sin


def halves(value):
    high = value.astype(BF16)
    return high, (value - high.astype(F32)).astype(BF16)


def iota(shape, axis):
    return lax.broadcasted_iota(I32, shape, axis)


def rotation(cos, sin, part_out, part_in):
    cross = jnp.where(part_out == 0, sin, -sin)
    return jnp.where(part_out == part_in, cos, cross)


def phase(name):
    pass


def kernel(codes_in, aperture_in, offsets_in, out, codes, aperture, offsets, yslots, xslots, zslots,
           p1s, p1r, gathered, tcos, tsin, wmat, emat, zsend, zrecv, fsend, landing,
           insem, ysend, yrecv, axsend, axrecv, azsend, azrecv, p1send, p1recv,
           p2send, p2recv, asend, arecv, bsend, brecv):
    y = lax.axis_index("row")
    col = lax.axis_index("col")
    core = col % NCORE
    z = (col // NCORE) % NZ
    x = col // (NCORE * NZ)
    me = x * NCORE + core

    def at_y(k):
        return (k, col)

    def at_b(k):
        return (y, ((k // NCORE) * NZ + z) * NCORE + k % NCORE)

    def at_z(k):
        return (y, (x * NZ + k) * NCORE + core)

    def remote(src, dst, ss, rs, where):
        return pltpu.make_async_remote_copy(
            src_ref=src, dst_ref=dst, send_sem=ss, recv_sem=rs,
            device_id=where, device_id_type=MESH)

    phase("start")
    barrier = pltpu.get_barrier_semaphore()

    @pl.loop(1, 8)
    def _(k):
        for where in (at_y((y + k) % NY), at_b((me + k) % NB), at_z((z + k) % NZ)):
            pl.semaphore_signal(barrier, inc=1, device_id=where, device_id_type=MESH)

    loads = [pltpu.make_async_copy(codes_in, codes, insem.at[0]),
             pltpu.make_async_copy(aperture_in, aperture, insem.at[1]),
             pltpu.make_async_copy(offsets_in, offsets, insem.at[2])]
    for load in loads:
        load.start()
    i, j = iota((512, 512), 0), iota((512, 512), 1)
    pick = jnp.where(i == 4 * (j & 127) + (j >> 7), 1.0, 0.0).astype(BF16)
    for load in loads:
        load.wait()

    phase("field")
    off0, off1 = offsets[:, 0:1], offsets[:, 1:2]
    opened = aperture[...]
    per_lane = jnp.sum(opened, axis=0, keepdims=True)
    count = sum(per_lane[:, j * 128:(j + 1) * 128] for j in range(4))
    yslots[y, 0:1, :] = jnp.broadcast_to(off0 + off1, (1, 128))
    yslots[y, 1:2, :] = count

    row = iota((ROWS, 512), 0)
    code = codes[...] + jnp.where(row < 16, off0, off0 + off1)
    code = code & 4095
    marked = jnp.concatenate([(code >> 6) + 64 * opened, code & 63], axis=0)
    moved = jnp.dot(marked.astype(F32).astype(BF16), pick, preferred_element_type=F32)
    moved = moved.astype(I32)
    high, low = moved[:ROWS], moved[ROWS:]
    amplitude = (high >> 6).astype(F32)
    cos, sin = cos_sin(((high & 63) << 6) + low, 12)
    field = (amplitude * cos, amplitude * sin)
    for b in range(NB):
        bx, bc = b // NCORE, b % NCORE
        for part in range(2):
            p1s[b * 32 + part * 16:b * 32 + part * 16 + 16, :] = (
                field[part][bc * HALF:(bc + 1) * HALF, bx * 128:(bx + 1) * 128])

    phase("barrier")
    pl.semaphore_wait(barrier, 21)

    phase("startp1")

    def y_copy(peer):
        return remote(yslots.at[y], yslots.at[y], ysend.at[peer], yrecv.at[y], at_y(peer))

    def p1_copy(peer):
        return remote(p1s.at[pl.ds(peer * 32, 32), :], p1r.at[pl.ds(me * 32, 32), :],
                      p1send.at[peer], p1recv.at[me], at_b(peer))

    @pl.loop(1, 8)
    def _(k):
        p1_copy((me + k) % NB).start()

    @pl.loop(1, 8)
    def _(k):
        y_copy((y + k) % NY).start()

    p1r[pl.ds(pl.multiple_of(me * 32, 32), 32), :] = p1s[pl.ds(pl.multiple_of(me * 32, 32), 32), :]

    phase("tables")
    shape = (512, 128)
    i, j = iota(shape, 0), iota(shape, 1)
    source = j & 7
    a = ((source >> 1) * NZ + ((j >> 3) & 7)) * NCORE + (source & 1)
    cos, sin = cos_sin(a * (i & 255), 8)
    w_high, w_low = halves(rotation(cos, sin, i >> 8, j >> 6))
    wmat[:, 0:128] = w_high
    wmat[:, 128:256] = w_high
    wmat[:, 256:384] = w_low
    shape = (256, 128)
    cos, sin = cos_sin((4 * iota(shape, 1) + x) * iota(shape, 0), 17)
    tcos[...] = cos
    tsin[...] = sin
    shape = (32, 256)
    i, j = iota(shape, 0), iota(shape, 1)
    q = 2 * (i >> 3) + ((i >> 1) & 1)
    d_low = NCORE * z + ((i >> 2) & 1)
    cos, sin = cos_sin((4 * (j & 127) + x) * (8 * d_low + q), 9)
    e_high, e_low = halves(rotation(cos, sin, i & 1, j >> 7))
    emat[0:32, :] = e_high
    emat[32:64, :] = e_low

    phase("p1wait")

    @pl.loop(1, 8)
    def _(k):
        peer = (me + k) % NB
        remote(p1s.at[pl.ds(peer * 32, 32), :], p1r.at[pl.ds(peer * 32, 32), :],
               p1send.at[peer], p1recv.at[peer], at_b(peer)).wait_recv()

    phase("relayout")
    for n in range(HALF):
        for part in range(2):
            gathered[z, n, part * 8:(part + 1) * 8, :] = (
                p1r[pl.ds(part * 16 + n, NB, stride=32), :])

    right, left = (z + 1) % NZ, (z + NZ - 1) % NZ

    def ring(block, group, way, step):
        part = gathered.at[block, pl.ds(group * GROWS, GROWS)]
        return remote(part, part, p2send.at[way, step, group], p2recv.at[block, group],
                      at_z(right if way == 0 else left))

    def ring_block(way, step):
        return (z + NZ - step) % NZ if way == 0 else (z + step) % NZ

    def forwards(way, step, group):
        return step < 3 or (group % 2 == 0) == (way == 0)

    def arrived(block, group):
        part = gathered.at[block, pl.ds(group * GROWS, GROWS)]
        remote(part, part, p2send.at[0, 0, group], p2recv.at[block, group],
               at_z(left)).wait_recv()

    def ring_step(step, group):
        for way in range(2):
            if step:
                arrived(ring_block(way, step), group)
            if forwards(way, step, group):
                ring(ring_block(way, step), group, way, step).start()

    def ax_copy(peer):
        return remote(xslots.at[me], xslots.at[me], axsend.at[peer], axrecv.at[me], at_b(peer))

    def az_copy(peer):
        return remote(zslots.at[z], zslots.at[z], azsend.at[peer], azrecv.at[z], at_z(peer))

    def small_y():
        @pl.loop(1, 8)
        def _(k):
            peer = (y + k) % NY
            remote(yslots.at[peer], yslots.at[peer], ysend.at[peer], yrecv.at[peer],
                   at_y(peer)).wait_recv()

        before = jnp.zeros((1, 128), I32)
        count = jnp.zeros((1, 128), I32)
        for k in range(NY):
            before = before + jnp.where(k < y, yslots[k, 0:1, :], 0)
            count = count + yslots[k, 1:2, :]
        xslots[me, 0:1, :] = before & 4095
        xslots[me, 1:2, :] = count

        @pl.loop(1, 8)
        def _(k):
            ax_copy((me + k) % NB).start()

    def small_x():
        @pl.loop(1, 8)
        def _(k):
            peer = (me + k) % NB
            remote(xslots.at[peer], xslots.at[peer], axsend.at[peer], axrecv.at[peer],
                   at_b(peer)).wait_recv()
        zslots[z, 0:8, :] = xslots[:, 0, :]
        zslots[z, 8:16, :] = xslots[:, 1, :]

        @pl.loop(1, 8)
        def _(k):
            az_copy((z + k) % NZ).start()

    known = []

    def small_z():
        @pl.loop(1, 8)
        def _(k):
            peer = (z + k) % NZ
            remote(zslots.at[peer], zslots.at[peer], azsend.at[peer], azrecv.at[peer],
                   at_z(peer)).wait_recv()
        total = jnp.sum(zslots[:, 8:16, :], axis=0)
        total = jnp.sum(jnp.sum(total.astype(F32), axis=0, keepdims=True), axis=1, keepdims=True)
        known.extend(cos_sin(zslots[:, 0:8, :], 12))
        known.append(jnp.sqrt(F32(ROWS * NY) / total))

    nt = (((1,), (1,)), ((), ()))

    def a_copy(g, peer):
        return remote(zsend.at[g, :, pl.ds(peer * 8 * GROWS, 8 * GROWS), :], zrecv.at[x, g],
                      asend.at[g, peer], arecv.at[g, x], at_b(peer * NCORE + core))

    def transform(g):
        pcos, psin = known[:2]
        for pair in range(GROWS // 2):
            columns = []
            for n in range(2):
                block = gathered[:, g * GROWS + pair * 2 + n]
                re, im = block[:, 0:8, :], block[:, 8:16, :]
                columns.append(jnp.concatenate(
                    [(re * pcos - im * psin).reshape(64, 128),
                     (re * psin + im * pcos).reshape(64, 128)], axis=0))
            high, low = halves(jnp.concatenate(columns, axis=1))
            spec = jnp.dot(wmat[...], jnp.concatenate([high, low, high], axis=0),
                           preferred_element_type=F32)
            for n in range(2):
                re = spec[0:256, n * 128:(n + 1) * 128]
                im = spec[256:512, n * 128:(n + 1) * 128]
                c, s = tcos[...], tsin[...]
                turned = jnp.concatenate([re * c + im * s, im * c - re * s], axis=1)
                high, low = halves(turned)
                first = lax.dot_general(emat[...], high, nt, preferred_element_type=F32)
                second = lax.dot_general(emat[0:32, :], low, nt, preferred_element_type=F32)
                result = first[0:32] + first[32:64] + second
                for h in range(2):
                    zsend[g, h, pl.ds(pair * 2 + n, 32, stride=GROWS), :] = (
                        result[:, h * 128:(h + 1) * 128])

    def finish(g):
        phase(f"fin{g}")
        arrived((z + 4) % NZ, g)
        if g == 0:
            phase("azwait")
            small_z()
        phase(f"dft{g}")
        transform(g)
        phase(f"asend{g}")
        for k in range(1, NX):
            a_copy(g, (x + k) % NX).start()
        zrecv[x, g] = zsend[g, :, pl.ds(pl.multiple_of(x * 8 * GROWS, 8 * GROWS), 8 * GROWS), :]

    def b_copy(g, peer):
        return remote(fsend.at[g, peer],
                      landing.at[core, g, :, pl.ds(pl.multiple_of(x * 512, 512), 512)],
                      bsend.at[g, peer], brecv.at[g, me], at_b(peer))

    def combine(g):
        phase(f"await{g}")
        for k in range(1, NX):
            peer = (x + k) % NX
            remote(zrecv.at[peer, g], zrecv.at[peer, g], asend.at[g, peer], arecv.at[g, peer],
                   at_b(peer * NCORE + core)).wait_recv()
        phase(f"dft4_{g}")
        scale = known[2]
        turn = jnp.where(iota((8, 128), 0) < GROWS, scale, -scale)
        for dc in range(2):
            for ql in range(2):
                for h in range(2):
                    start = (dc * 2 + ql) * 8
                    t = [zrecv[b, g, h, start:start + 8, :] for b in range(NX)]
                    even, odd = (t[0] + t[2]) * scale, (t[1] + t[3]) * scale
                    differ = (t[0] - t[2]) * scale
                    turned = pltpu.roll(t[1] - t[3], GROWS, axis=0) * turn
                    results = (even + odd, differ + turned, even - odd, differ - turned)
                    for dx in range(NX):
                        fsend[g, dx * NCORE + dc, :, (ql * 2 + h) * 128:(ql * 2 + h + 1) * 128] = results[dx]

        @pl.loop(1, 8)
        def _(k):
            b_copy(g, (me + k) % NB).start()
        landing[core, g, :, pl.ds(pl.multiple_of(x * 512, 512), 512)] = fsend[g, me]

    def deliver(g):
        phase(f"bwait{g}")

        @pl.loop(1, 8)
        def _(k):
            peer = (me + k) % NB
            spot = landing.at[peer % NCORE, g, :, pl.ds(pl.multiple_of((peer // NCORE) * 512, 512), 512)]
            remote(spot, spot, bsend.at[g, peer], brecv.at[g, peer], at_b(peer)).wait_recv()
        phase(f"out{g}")
        for c in range(NCORE):
            for p in range(2):
                out[p, c * HALF + g * GROWS:c * HALF + (g + 1) * GROWS, :] = (
                    landing[c, g, p * GROWS:(p + 1) * GROWS, :])

    for _, name, work in sorted(schedule(ring_step, finish, combine, deliver, small_y, small_x),
                                key=lambda e: e[0]):
        phase(name)
        work()

    phase("drain")

    @pl.loop(1, 8)
    def _(k):
        y_copy((y + k) % NY).wait_send()
        p1_copy((me + k) % NB).wait_send()
        ax_copy((me + k) % NB).wait_send()
        az_copy((z + k) % NZ).wait_send()
        for g in range(GROUPS):
            b_copy(g, (me + k) % NB).wait_send()
    for step in range(4):
        for g in range(GROUPS):
            for way in range(2):
                if forwards(way, step, g):
                    ring(ring_block(way, step), g, way, step).wait_send()
    for g in range(GROUPS):
        for k in range(1, NX):
            a_copy(g, (x + k) % NX).wait_send()
    phase(None)


def schedule(ring_step, finish, combine, deliver, small_y, small_x):
    hop, lag, fin, exch = PACE
    part = functools.partial
    events = [(SMALL[0], "ysmall", small_y), (SMALL[1], "xsmall", small_x)]
    for g in range(GROUPS):
        for step in range(4):
            events.append((hop * step + lag * g, f"r{step}{g}", part(ring_step, step, g)))
        done = hop * 4 + fin * g
        events.append((done, f"fin{g}", part(finish, g)))
        events.append((done + exch, f"await{g}", part(combine, g)))
        events.append((done + 2 * exch + 10.0, f"bwait{g}", part(deliver, g)))
    return events


PACE = (2.2, 1.0, 1.2, 5.0)
SMALL = (2.9, 5.3)


def per_device(phase_codes, aperture, tile_offsets):
    dma = pltpu.SemaphoreType.DMA
    vmem = pltpu.VMEM
    return pl.pallas_call(
        kernel,
        out_shape=pltpu.VMEM((2, ROWS, 2048), F32),
        in_specs=[pl.BlockSpec(memory_space=pl.ANY)] * 3,
        out_specs=pl.BlockSpec(memory_space=pltpu.VMEM),
        scratch_shapes=[
            vmem((ROWS, 512), I32), vmem((ROWS, 512), I32), vmem((1, 2), I32),
            vmem((NY, 2, 128), I32), vmem((NB, 2, 128), I32), vmem((NZ, 16, 128), I32),
            vmem((NB * 32, 128), F32), vmem((NB * 32, 128), F32),
            vmem((NZ, HALF, 16, 128), F32),
            vmem((256, 128), F32), vmem((256, 128), F32),
            vmem((512, 384), BF16), vmem((64, 256), BF16),
            vmem((GROUPS, 2, 32 * GROWS, 128), F32),
            vmem((NX, GROUPS, 2, 8 * GROWS, 128), F32),
            vmem((GROUPS, NB, 2 * GROWS, 512), F32),
            vmem((NCORE, GROUPS, 2 * GROWS, 2048), F32),
            dma((3,)),
            dma((NY,)), dma((NY,)), dma((NB,)), dma((NB,)), dma((NZ,)), dma((NZ,)),
            dma((NB,)), dma((NB,)),
            dma((2, 4, GROUPS)), dma((NZ, GROUPS)),
            dma((GROUPS, NX)), dma((GROUPS, NX)), dma((GROUPS, NB)), dma((GROUPS, NB)),
        ],
        compiler_params=pltpu.CompilerParams(collective_id=0, has_side_effects=True),
    )(phase_codes, aperture, tile_offsets.reshape(1, 2))


def solution(mesh):
    placed = (P("row", "col"), P("row", "col"), P("row", "col"))
    return jax.shard_map(
        per_device, mesh=mesh, in_specs=placed, out_specs=P(None, "row", "col"), check_vma=False
    )
```

time: 60.4 us -> 51.6 us (0.85)
  Pallas kernels: 57 us -> 50.6 us
  local copies, waits for them, and re-layouts: 3.17 us -> 0.8 us
    pallas_call x1, Pallas kernels: 57 us -> 50.6 us  [per_device(): pl.pallas_call(kernel, out_shape=pltpu.VMEM((2, ROWS, 2048), F32), in_spe...]
    unnamed x2 -> x1, local copies, waits for them, and re-layouts: 3.17 us -> 0.8 us
where the time goes in v2:
time: 51.6 us; the launch traced here: 51.4 us
  Pallas kernels  50.6 us (98%)
  local copies, waits for them, and re-layouts  0.8 us (2%)
    pallas_call x1, Pallas kernels, per_device(): pl.pallas_call(kernel, out_shape=pltpu.VMEM((2, ROWS, 2048), F32), in_spe...  50.6 us

profile of v2, /device:TPU:1, one launch (start us, length us, event | category | flops | bytes accessed | tf_op | source)
XLA Modules:
  0.0 51.4 jit_solution(3451098337961232498)
XLA Ops:
  0.0 50.6 %shard_map.37 = f32[2,32,2048]{2,1,0:T(8,128)S(1)} custom-call(s32[32,512]{1,0:T(8,128)} %codes_in.1, s32[32,512]{1,0:T(8,128)} %aperture_in.1, s32[1,2]{1,0:T(1,128)} %bitcast.1), custom_call_target="tpu_custom_call" | custom-call | tf_op jit(solution)/shard_map/pallas_call | solution.py:397
  50.6 0.8 %copy.5 = f32[2,32,2048]{2,1,0:T(8,128)} copy(f32[2,32,2048]{2,1,0:T(8,128)S(1)} %shard_map.37) | data formatting | bytes 1048576

commit v3 on v2

v3 whole, which is shorter than its diff:
```python
import functools
import math

import jax
import jax.numpy as jnp
from jax import lax
from jax.experimental import pallas as pl
from jax.experimental.pallas import tpu as pltpu
from jax.sharding import PartitionSpec as P

MESH = pl.DeviceIdType.MESH
F32, I32, BF16 = jnp.float32, jnp.int32, jnp.bfloat16

NY, NX, NZ, NCORE = 8, 4, 8, 2
NB = NX * NCORE
ROWS = 32
HALF = 16
MSG = 40
GROUPS = 4
GROWS = HALF // GROUPS


def cos_sin(index, bits):
    size = 1 << bits
    index = index & (size - 1)
    quadrant = (index + (size >> 3)) >> (bits - 2)
    rest = index - (quadrant << (bits - 2))
    x = rest.astype(F32) * F32(2.0 * math.pi / size)
    y = x * x
    s = x * (1.0 + y * (-1.0 / 6 + y * (1.0 / 120 + y * (-1.0 / 5040 + y * (1.0 / 362880)))))
    c = 1.0 + y * (-0.5 + y * (1.0 / 24 + y * (-1.0 / 720 + y * (1.0 / 40320))))
    quadrant = quadrant & 3
    swap = (quadrant & 1) == 1
    cos = jnp.where(swap, s, c)
    sin = jnp.where(swap, c, s)
    cos = jnp.where((quadrant == 1) | (quadrant == 2), -cos, cos)
    sin = jnp.where(quadrant >= 2, -sin, sin)
    return cos, sin


def halves(value):
    high = value.astype(BF16)
    return high, (value - high.astype(F32)).astype(BF16)


def iota(shape, axis):
    return lax.broadcasted_iota(I32, shape, axis)


def rotation(cos, sin, part_out, part_in):
    cross = jnp.where(part_out == 0, sin, -sin)
    return jnp.where(part_out == part_in, cos, cross)


def phase(name):
    pass


def kernel(codes_in, aperture_in, offsets_in, out, codes, aperture, offsets, yslots, zslots, cslots,
           p1s, p1r, gathered, tcos, tsin, wmat, emat, zsend, zrecv, fsend, landing,
           ready_y, ready_z, insem, p1send, p1recv, ysend, yrecv, azsend, azrecv, csend, crecv,
           p2send, p2recv, asend, arecv, bsend, brecv):
    y = lax.axis_index("row")
    col = lax.axis_index("col")
    core = col % NCORE
    z = (col // NCORE) % NZ
    x = col // (NCORE * NZ)
    me = x * NCORE + core

    def at_y(k):
        return (k, col)

    def at_b(k):
        return (y, ((k // NCORE) * NZ + z) * NCORE + k % NCORE)

    def at_z(k):
        return (y, (x * NZ + k) * NCORE + core)

    def remote(src, dst, ss, rs, where):
        return pltpu.make_async_remote_copy(
            src_ref=src, dst_ref=dst, send_sem=ss, recv_sem=rs,
            device_id=where, device_id_type=MESH)

    phase("start")
    barrier = pltpu.get_barrier_semaphore()

    def signal(semaphore, where):
        pl.semaphore_signal(semaphore, inc=1, device_id=where, device_id_type=MESH)

    partners = [((x + dx) % NX) * NCORE + (core + dc) % NCORE
                for dx, dc in ((2, 0), (2, 1), (1, 0), (3, 0), (1, 1), (3, 1), (0, 1))]
    right, left = (z + 1) % NZ, (z + NZ - 1) % NZ
    for peer in partners:
        signal(barrier, at_b(peer))
    for peer in (right, left):
        signal(barrier, at_z(peer))
    for k in range(2, NZ - 1):
        peer = (z + k) % NZ

        @pl.when(peer > z)
        def _():
            signal(barrier, at_z(peer))

    @pl.loop(y + 1, NY)
    def _(k):
        signal(barrier, at_y(k))

    loads = [pltpu.make_async_copy(codes_in, codes, insem.at[0]),
             pltpu.make_async_copy(aperture_in, aperture, insem.at[1]),
             pltpu.make_async_copy(offsets_in, offsets, insem.at[2])]
    for load in loads:
        load.start()
    i, j = iota((512, 512), 0), iota((512, 512), 1)
    pick = jnp.where(i == 4 * (j & 127) + (j >> 7), 1.0, 0.0).astype(BF16)
    for load in loads:
        load.wait()

    phase("field")
    off0, off1 = offsets[:, 0:1], offsets[:, 1:2]
    opened = aperture[...]
    per_lane = jnp.sum(opened, axis=0, keepdims=True)
    count = sum(per_lane[:, j * 128:(j + 1) * 128] for j in range(4))
    total = jnp.broadcast_to(off0 + off1, (1, 128)).astype(F32)
    count = count.astype(F32)

    row = iota((ROWS, 512), 0)
    code = codes[...] + jnp.where(row < 16, off0, off0 + off1)
    code = code & 4095
    marked = jnp.concatenate([(code >> 6) + 64 * opened, code & 63], axis=0)
    moved = jnp.dot(marked.astype(F32).astype(BF16), pick, preferred_element_type=F32)
    moved = moved.astype(I32)
    high, low = moved[:ROWS], moved[ROWS:]
    amplitude = (high >> 6).astype(F32)
    cos, sin = cos_sin(((high & 63) << 6) + low, 12)
    field = (amplitude * cos, amplitude * sin)
    for b in range(NB):
        bx, bc = b // NCORE, b % NCORE
        for part in range(2):
            p1s[b * MSG + part * 16:b * MSG + part * 16 + 16, :] = (
                field[part][bc * HALF:(bc + 1) * HALF, bx * 128:(bx + 1) * 128])
        p1s[b * MSG + 32:b * MSG + 33, :] = total
        p1s[b * MSG + 33:b * MSG + 34, :] = count

    phase("barrier")
    entered_z = z - (z + 6) // 7 - z // 7
    pl.semaphore_wait(barrier, 9 + entered_z + y)

    phase("startp1")

    def p1_copy(peer):
        return remote(p1s.at[pl.ds(peer * MSG, MSG), :], p1r.at[pl.ds(me * MSG, MSG), :],
                      p1send, p1recv, at_b(peer))

    for peer in partners:
        p1_copy(peer).start()
    for k in range(2, NZ - 1):
        peer = (z + k) % NZ

        @pl.when(peer < z)
        def _():
            signal(ready_z, at_z(peer))

    @pl.loop(0, y)
    def _(k):
        signal(ready_y, at_y(k))

    own = pl.ds(pl.multiple_of(me * MSG, MSG), MSG)
    p1r[own, :] = p1s[own, :]

    phase("tables")
    shape = (512, 128)
    i, j = iota(shape, 0), iota(shape, 1)
    source = j & 7
    a = ((source >> 1) * NZ + ((j >> 3) & 7)) * NCORE + (source & 1)
    cos, sin = cos_sin(a * (i & 255), 8)
    w_high, w_low = halves(rotation(cos, sin, i >> 8, j >> 6))
    wmat[:, 0:128] = w_high
    wmat[:, 128:256] = w_high
    wmat[:, 256:384] = w_low
    shape = (256, 128)
    cos, sin = cos_sin((4 * iota(shape, 1) + x) * iota(shape, 0), 17)
    tcos[...] = cos
    tsin[...] = sin
    shape = (32, 256)
    i, j = iota(shape, 0), iota(shape, 1)
    q = 2 * (i >> 3) + ((i >> 1) & 1)
    d_low = NCORE * z + ((i >> 2) & 1)
    cos, sin = cos_sin((4 * (j & 127) + x) * (8 * d_low + q), 9)
    e_high, e_low = halves(rotation(cos, sin, i & 1, j >> 7))
    emat[0:32, :] = e_high
    emat[32:64, :] = e_low

    phase("p1wait")
    seven = pl.ds(0, 7 * MSG)
    remote(p1s.at[seven, :], p1r.at[seven, :], p1send, p1recv, at_z(right)).wait_recv()

    phase("relayout")
    for n in range(HALF):
        for part in range(2):
            gathered[z, n, part * 8:(part + 1) * 8, :] = (
                p1r[pl.ds(part * 16 + n, NB, stride=MSG), :])

    def ring(block, group, way, step):
        part = gathered.at[block, pl.ds(group * GROWS, GROWS)]
        return remote(part, part, p2send, p2recv.at[block, group],
                      at_z(right if way == 0 else left))

    def ring_block(way, step):
        return (z + NZ - step) % NZ if way == 0 else (z + step) % NZ

    def forwards(way, step, group):
        return step < 3 or (group % 2 == 0) == (way == 0)

    def arrived(block, group):
        part = gathered.at[block, pl.ds(group * GROWS, GROWS)]
        remote(part, part, p2send, p2recv.at[block, group],
               at_z(left)).wait_recv()

    def ring_step(step, group):
        for way in range(2):
            if step:
                arrived(ring_block(way, step), group)
            if forwards(way, step, group):
                ring(ring_block(way, step), group, way, step).start()

    def y_copy(peer, slot):
        return remote(yslots.at[slot], yslots.at[slot], ysend.at[peer], yrecv.at[slot], at_y(peer))

    def az_copy(peer):
        return remote(zslots.at[z], zslots.at[z], azsend, azrecv, at_z(peer))

    def c_copy(peer):
        return remote(cslots.at[y], cslots.at[y], csend, crecv, at_y(peer))

    def small_y():
        yslots[y] = p1r[pl.ds(32, NB, stride=MSG), :]
        @pl.when(y < NY - 1)
        def _():
            pl.semaphore_wait(ready_y, NY - 1 - y)

        @pl.loop(y + 1, NY)
        def _(k):
            y_copy(k, y).start()

    def small_z():
        @pl.loop(0, y)
        def _(k):
            y_copy(k, k).wait_recv()
        before = lax.fori_loop(0, y, lambda k, acc: acc + yslots[k], jnp.zeros((NB, 128), F32))
        zslots[z, 0:8, :] = before
        zslots[z, 8:16, :] = p1r[pl.ds(33, NB, stride=MSG), :]
        @pl.when(z < NZ - 2)
        def _():
            pl.semaphore_wait(ready_z, 5 + (z + 6) // 7 - z)

        @pl.loop(1, NZ)
        def _(k):
            az_copy((z + k) % NZ).start()

    known = []

    def prefix():
        remote(zslots.at[pl.ds(0, 7)], zslots.at[pl.ds(0, 7)], azsend, azrecv, at_z(right)).wait_recv()
        known.extend(cos_sin(zslots[:, 0:8, :].astype(I32), 12))
        cslots[y] = jnp.sum(zslots[:, 8:16, :], axis=0)

        @pl.loop(1, NY)
        def _(k):
            c_copy((y + k) % NY).start()

    def normalization():
        remote(cslots.at[pl.ds(0, 7)], cslots.at[pl.ds(0, 7)], csend, crecv, at_z(right)).wait_recv()
        total = jnp.sum(cslots[...], axis=0)
        total = jnp.sum(jnp.sum(total, axis=0, keepdims=True), axis=1, keepdims=True)
        known.append(jnp.sqrt(F32(ROWS * NY) / total))

    nt = (((1,), (1,)), ((), ()))

    def a_copy(g, peer):
        return remote(zsend.at[g, :, pl.ds(peer * 8 * GROWS, 8 * GROWS), :], zrecv.at[x, g],
                      asend, arecv.at[g], at_b(peer * NCORE + core))

    def transform(g):
        pcos, psin = known[:2]
        for pair in range(GROWS // 2):
            columns = []
            for n in range(2):
                block = gathered[:, g * GROWS + pair * 2 + n]
                re, im = block[:, 0:8, :], block[:, 8:16, :]
                columns.append(jnp.concatenate(
                    [(re * pcos - im * psin).reshape(64, 128),
                     (re * psin + im * pcos).reshape(64, 128)], axis=0))
            high, low = halves(jnp.concatenate(columns, axis=1))
            spec = jnp.dot(wmat[...], jnp.concatenate([high, low, high], axis=0),
                           preferred_element_type=F32)
            for n in range(2):
                re = spec[0:256, n * 128:(n + 1) * 128]
                im = spec[256:512, n * 128:(n + 1) * 128]
                c, s = tcos[...], tsin[...]
                turned = jnp.concatenate([re * c + im * s, im * c - re * s], axis=1)
                high, low = halves(turned)
                first = lax.dot_general(emat[...], high, nt, preferred_element_type=F32)
                second = lax.dot_general(emat[0:32, :], low, nt, preferred_element_type=F32)
                result = first[0:32] + first[32:64] + second
                for h in range(2):
                    zsend[g, h, pl.ds(pair * 2 + n, 32, stride=GROWS), :] = (
                        result[:, h * 128:(h + 1) * 128])

    def finish(g):
        phase(f"fin{g}")
        arrived((z + 4) % NZ, g)
        if g == 0:
            phase("azwait")
            prefix()
        phase(f"dft{g}")
        transform(g)
        phase(f"asend{g}")
        for k in (2, 1, 3):
            a_copy(g, (x + k) % NX).start()
        zrecv[x, g] = zsend[g, :, pl.ds(pl.multiple_of(x * 8 * GROWS, 8 * GROWS), 8 * GROWS), :]

    def b_copy(g, peer):
        return remote(fsend.at[g, peer],
                      landing.at[core, g, :, pl.ds(pl.multiple_of(x * 512, 512), 512)],
                      bsend, brecv.at[g], at_b(peer))

    def combine(g):
        phase(f"await{g}")
        remote(zrecv.at[pl.ds(0, 3), g], zrecv.at[pl.ds(0, 3), g], asend, arecv.at[g],
               at_z(right)).wait_recv()
        phase(f"dft4_{g}")
        turn = jnp.where(iota((8, 128), 0) < GROWS, F32(1.0), F32(-1.0))
        for dc in range(2):
            for ql in range(2):
                for h in range(2):
                    start = (dc * 2 + ql) * 8
                    t = [zrecv[b, g, h, start:start + 8, :] for b in range(NX)]
                    even, odd = t[0] + t[2], t[1] + t[3]
                    differ = t[0] - t[2]
                    turned = pltpu.roll(t[1] - t[3], GROWS, axis=0) * turn
                    results = (even + odd, differ + turned, even - odd, differ - turned)
                    for dx in range(NX):
                        fsend[g, dx * NCORE + dc, :, (ql * 2 + h) * 128:(ql * 2 + h + 1) * 128] = results[dx]

        for peer in partners:
            b_copy(g, peer).start()
        landing[core, g, :, pl.ds(pl.multiple_of(x * 512, 512), 512)] = fsend[g, me]

    def deliver(g):
        phase(f"bwait{g}")

        remote(fsend.at[g, pl.ds(0, 7)], fsend.at[g, pl.ds(0, 7)], bsend, brecv.at[g],
               at_z(right)).wait_recv()
        if g == 0:
            phase("cwait")
            normalization()
        phase(f"out{g}")
        scale = known[2]
        for c in range(NCORE):
            for p in range(2):
                out[p, c * HALF + g * GROWS:c * HALF + (g + 1) * GROWS, :] = (
                    landing[c, g, p * GROWS:(p + 1) * GROWS, :] * scale)

    for _, name, work in sorted(schedule(ring_step, finish, combine, deliver, small_y, small_z),
                                key=lambda e: e[0]):
        phase(name)
        work()

    phase("drain")

    @pl.loop(y + 1, NY)
    def _(k):
        y_copy(k, y).wait_send()

    for ref, semaphore in ((p1s.at[seven, :], p1send), (zslots.at[pl.ds(0, 7)], azsend),
                           (cslots.at[pl.ds(0, 7)], csend), (gathered.at[pl.ds(0, 7)], p2send),
                           (zrecv.at[pl.ds(0, 3)], asend), (fsend.at[:, pl.ds(0, 7)], bsend)):
        remote(ref, ref, semaphore, p1recv, at_z(right)).wait_send()
    phase(None)


def schedule(ring_step, finish, combine, deliver, small_y, small_z):
    hop, lag, fin, exch = PACE
    part = functools.partial
    events = [(SMALL[0], "ysmall", small_y), (SMALL[1], "zsmall", small_z)]
    for g in range(GROUPS):
        for step in range(4):
            events.append((hop * step + lag * g, f"r{step}{g}", part(ring_step, step, g)))
        done = hop * 4 + fin * g
        events.append((done, f"fin{g}", part(finish, g)))
        events.append((done + exch, f"await{g}", part(combine, g)))
        events.append((done + 2 * exch + 10.0, f"bwait{g}", part(deliver, g)))
    return events


PACE = (2.2, 1.0, 1.2, 5.0)
SMALL = (0.5, 3.3)


def per_device(phase_codes, aperture, tile_offsets):
    dma = pltpu.SemaphoreType.DMA
    vmem = pltpu.VMEM
    return pl.pallas_call(
        kernel,
        out_shape=pltpu.VMEM((2, ROWS, 2048), F32),
        in_specs=[pl.BlockSpec(memory_space=pl.ANY)] * 3,
        out_specs=pl.BlockSpec(memory_space=pltpu.VMEM),
        scratch_shapes=[
            vmem((ROWS, 512), I32), vmem((ROWS, 512), I32), vmem((1, 2), I32),
            vmem((NY, NB, 128), F32), vmem((NZ, 16, 128), F32), vmem((NY, NB, 128), F32),
            vmem((NB * MSG, 128), F32), vmem((NB * MSG, 128), F32),
            vmem((NZ, HALF, 16, 128), F32),
            vmem((256, 128), F32), vmem((256, 128), F32),
            vmem((512, 384), BF16), vmem((64, 256), BF16),
            vmem((GROUPS, 2, 32 * GROWS, 128), F32),
            vmem((NX, GROUPS, 2, 8 * GROWS, 128), F32),
            vmem((GROUPS, NB, 2 * GROWS, 512), F32),
            vmem((NCORE, GROUPS, 2 * GROWS, 2048), F32),
            pltpu.SemaphoreType.REGULAR, pltpu.SemaphoreType.REGULAR, dma((3,)),
            dma, dma, dma((NY,)), dma((NY,)), dma, dma, dma, dma,
            dma, dma((NZ, GROUPS)), dma, dma((GROUPS,)), dma, dma((GROUPS,)),
        ],
        compiler_params=pltpu.CompilerParams(collective_id=0, has_side_effects=True),
    )(phase_codes, aperture, tile_offsets.reshape(1, 2))


def solution(mesh):
    placed = (P("row", "col"), P("row", "col"), P("row", "col"))
    return jax.shard_map(
        per_device, mesh=mesh, in_specs=placed, out_specs=P(None, "row", "col"), check_vma=False
    )
```

time: 51.6 us -> 45.9 us (0.89)
  Pallas kernels: 50.6 us -> 44.9 us
    pallas_call x1, Pallas kernels: 50.6 us -> 44.9 us  [per_device(): pl.pallas_call(kernel, out_shape=pltpu.VMEM((2, ROWS, 2048), F32), in_spe...]
where the time goes in v3:
time: 45.9 us; the launch traced here: 45.7 us
  Pallas kernels  44.9 us (98%)
  local copies, waits for them, and re-layouts  0.8 us (2%)
    pallas_call x1, Pallas kernels, per_device(): pl.pallas_call(kernel, out_shape=pltpu.VMEM((2, ROWS, 2048), F32), in_spe...  44.9 us

profile of v3, /device:TPU:1, one launch (start us, length us, event | category | flops | bytes accessed | tf_op | source)
XLA Modules:
  0.0 45.7 jit_solution(16941675276879787224)
XLA Ops:
  0.0 44.9 %shard_map.37 = f32[2,32,2048]{2,1,0:T(8,128)S(1)} custom-call(s32[32,512]{1,0:T(8,128)} %codes_in.1, s32[32,512]{1,0:T(8,128)} %aperture_in.1, s32[1,2]{1,0:T(1,128)} %bitcast.1), custom_call_target="tpu_custom_call" | custom-call | tf_op jit(solution)/shard_map/pallas_call | solution.py:403
  45.0 0.8 %copy.5 = f32[2,32,2048]{2,1,0:T(8,128)} copy(f32[2,32,2048]{2,1,0:T(8,128)S(1)} %shard_map.37) | data formatting | bytes 1048576

commit v4 on v3

--- a/solution.py
+++ b/solution.py
@@ -15,7 +15,6 @@
 NB = NX * NCORE
 ROWS = 32
 HALF = 16
-MSG = 40
 GROUPS = 4
 GROWS = HALF // GROUPS
 
@@ -56,9 +55,9 @@
     pass
 
 
-def kernel(codes_in, aperture_in, offsets_in, out, codes, aperture, offsets, yslots, zslots, cslots,
+def kernel(codes_in, aperture_in, offsets_in, out, codes, aperture, offsets, xslots, yslots, zslots, cslots,
            p1s, p1r, gathered, tcos, tsin, wmat, emat, zsend, zrecv, fsend, landing,
-           ready_y, ready_z, insem, p1send, p1recv, ysend, yrecv, azsend, azrecv, csend, crecv,
+           ready_y, ready_z, insem, p1send, p1recv, xsend, xrecv, ysend, yrecv, azsend, azrecv, csend, crecv,
            p2send, p2recv, asend, arecv, bsend, brecv):
     y = lax.axis_index("row")
     col = lax.axis_index("col")
@@ -136,10 +135,12 @@
     for b in range(NB):
         bx, bc = b // NCORE, b % NCORE
         for part in range(2):
-            p1s[b * MSG + part * 16:b * MSG + part * 16 + 16, :] = (
-                field[part][bc * HALF:(bc + 1) * HALF, bx * 128:(bx + 1) * 128])
-        p1s[b * MSG + 32:b * MSG + 33, :] = total
-        p1s[b * MSG + 33:b * MSG + 34, :] = count
+            for g in range(GROUPS):
+                first = bc * HALF + g * GROWS
+                p1s[g, b * 8 + part * GROWS:b * 8 + (part + 1) * GROWS, :] = (
+                    field[part][first:first + GROWS, bx * 128:(bx + 1) * 128])
+    xslots[me, 0:1, :] = total
+    xslots[me, 1:2, :] = count
 
     phase("barrier")
     entered_z = z - (z + 6) // 7 - z // 7
@@ -147,12 +148,18 @@
 
     phase("startp1")
 
-    def p1_copy(peer):
-        return remote(p1s.at[pl.ds(peer * MSG, MSG), :], p1r.at[pl.ds(me * MSG, MSG), :],
-                      p1send, p1recv, at_b(peer))
+    def p1_copy(g, peer):
+        return remote(p1s.at[g, pl.ds(pl.multiple_of(peer * 8, 8), 8), :],
+                      p1r.at[g, pl.ds(pl.multiple_of(me * 8, 8), 8), :],
+                      p1send, p1recv.at[g], at_b(peer))
 
     for peer in partners:
-        p1_copy(peer).start()
+        p1_copy(0, peer).start()
+    for peer in partners:
+        remote(xslots.at[me], xslots.at[me], xsend, xrecv, at_b(peer)).start()
+    for g in range(1, GROUPS):
+        for peer in partners:
+            p1_copy(g, peer).start()
     for k in range(2, NZ - 1):
         peer = (z + k) % NZ
 
@@ -164,8 +171,9 @@
     def _(k):
         signal(ready_y, at_y(k))
 
-    own = pl.ds(pl.multiple_of(me * MSG, MSG), MSG)
-    p1r[own, :] = p1s[own, :]
+    own = pl.ds(pl.multiple_of(me * 8, 8), 8)
+    for g in range(GROUPS):
+        p1r[g, own, :] = p1s[g, own, :]
 
     phase("tables")
     shape = (512, 128)
@@ -190,15 +198,13 @@
     emat[0:32, :] = e_high
     emat[32:64, :] = e_low
 
-    phase("p1wait")
-    seven = pl.ds(0, 7 * MSG)
-    remote(p1s.at[seven, :], p1r.at[seven, :], p1send, p1recv, at_z(right)).wait_recv()
-
-    phase("relayout")
-    for n in range(HALF):
-        for part in range(2):
-            gathered[z, n, part * 8:(part + 1) * 8, :] = (
-                p1r[pl.ds(part * 16 + n, NB, stride=MSG), :])
+    def receive(g):
+        messages = p1r.at[g, pl.ds(0, 56), :]
+        remote(messages, messages, p1send, p1recv.at[g], at_z(right)).wait_recv()
+        for n in range(GROWS):
+            for part in range(2):
+                gathered[z, g * GROWS + n, part * 8:(part + 1) * 8, :] = (
+                    p1r[g, pl.ds(part * GROWS + n, NB, stride=8), :])
 
     def ring(block, group, way, step):
         part = gathered.at[block, pl.ds(group * GROWS, GROWS)]
@@ -217,6 +223,8 @@
                at_z(left)).wait_recv()
 
     def ring_step(step, group):
+        if step == 0:
+            receive(group)
         for way in range(2):
             if step:
                 arrived(ring_block(way, step), group)
@@ -233,7 +241,8 @@
         return remote(cslots.at[y], cslots.at[y], csend, crecv, at_y(peer))
 
     def small_y():
-        yslots[y] = p1r[pl.ds(32, NB, stride=MSG), :]
+        remote(xslots.at[pl.ds(0, 7)], xslots.at[pl.ds(0, 7)], xsend, xrecv, at_z(right)).wait_recv()
+        yslots[y] = xslots[:, 0, :]
         @pl.when(y < NY - 1)
         def _():
             pl.semaphore_wait(ready_y, NY - 1 - y)
@@ -248,7 +257,7 @@
             y_copy(k, k).wait_recv()
         before = lax.fori_loop(0, y, lambda k, acc: acc + yslots[k], jnp.zeros((NB, 128), F32))
         zslots[z, 0:8, :] = before
-        zslots[z, 8:16, :] = p1r[pl.ds(33, NB, stride=MSG), :]
+        zslots[z, 8:16, :] = xslots[:, 1, :]
         @pl.when(z < NZ - 2)
         def _():
             pl.semaphore_wait(ready_z, 5 + (z + 6) // 7 - z)
@@ -372,29 +381,32 @@
     def _(k):
         y_copy(k, y).wait_send()
 
-    for ref, semaphore in ((p1s.at[seven, :], p1send), (zslots.at[pl.ds(0, 7)], azsend),
+    for ref, semaphore in ((p1s.at[:, pl.ds(0, 56), :], p1send), (xslots.at[pl.ds(0, 7)], xsend),
+                           (zslots.at[pl.ds(0, 7)], azsend),
                            (cslots.at[pl.ds(0, 7)], csend), (gathered.at[pl.ds(0, 7)], p2send),
                            (zrecv.at[pl.ds(0, 3)], asend), (fsend.at[:, pl.ds(0, 7)], bsend)):
-        remote(ref, ref, semaphore, p1recv, at_z(right)).wait_send()
+        remote(ref, ref, semaphore, xrecv, at_z(right)).wait_send()
     phase(None)
 
 
 def schedule(ring_step, finish, combine, deliver, small_y, small_z):
-    hop, lag, fin, exch = PACE
     part = functools.partial
     events = [(SMALL[0], "ysmall", small_y), (SMALL[1], "zsmall", small_z)]
     for g in range(GROUPS):
         for step in range(4):
-            events.append((hop * step + lag * g, f"r{step}{g}", part(ring_step, step, g)))
-        done = hop * 4 + fin * g
-        events.append((done, f"fin{g}", part(finish, g)))
-        events.append((done + exch, f"await{g}", part(combine, g)))
-        events.append((done + 2 * exch + 10.0, f"bwait{g}", part(deliver, g)))
+            events.append((RING[step] + g * LAG, f"r{step}{g}", part(ring_step, step, g)))
+    for g in range(GROUPS):
+        events.append((FIN[g], f"fin{g}", part(finish, g)))
+        events.append((FOUR[g], f"await{g}", part(combine, g)))
+        events.append((100.0 + g, f"bwait{g}", part(deliver, g)))
     return events
 
 
-PACE = (2.2, 1.0, 1.2, 5.0)
-SMALL = (0.5, 3.3)
+RING = (0.0, 2.2, 4.4, 6.6)
+LAG = 1.0
+SMALL = (2.3, 6.0)
+FIN = (8.8, 10.0, 11.2, 12.4)
+FOUR = (13.5, 15.0, 16.5, 18.0)
 
 
 def per_device(phase_codes, aperture, tile_offsets):
@@ -407,8 +419,8 @@
         out_specs=pl.BlockSpec(memory_space=pltpu.VMEM),
         scratch_shapes=[
             vmem((ROWS, 512), I32), vmem((ROWS, 512), I32), vmem((1, 2), I32),
-            vmem((NY, NB, 128), F32), vmem((NZ, 16, 128), F32), vmem((NY, NB, 128), F32),
-            vmem((NB * MSG, 128), F32), vmem((NB * MSG, 128), F32),
+            vmem((NB, 2, 128), F32), vmem((NY, NB, 128), F32), vmem((NZ, 16, 128), F32), vmem((NY, NB, 128), F32),
+            vmem((GROUPS, NB * 8, 128), F32), vmem((GROUPS, NB * 8, 128), F32),
             vmem((NZ, HALF, 16, 128), F32),
             vmem((256, 128), F32), vmem((256, 128), F32),
             vmem((512, 384), BF16), vmem((64, 256), BF16),
@@ -417,7 +429,7 @@
             vmem((GROUPS, NB, 2 * GROWS, 512), F32),
             vmem((NCORE, GROUPS, 2 * GROWS, 2048), F32),
             pltpu.SemaphoreType.REGULAR, pltpu.SemaphoreType.REGULAR, dma((3,)),
-            dma, dma, dma((NY,)), dma((NY,)), dma, dma, dma, dma,
+            dma, dma((GROUPS,)), dma, dma, dma((NY,)), dma((NY,)), dma, dma, dma, dma,
             dma, dma((NZ, GROUPS)), dma, dma((GROUPS,)), dma, dma((GROUPS,)),
         ],
         compiler_params=pltpu.CompilerParams(collective_id=0, has_side_effects=True),

time: 45.9 us -> 44.5 us (0.969)
  Pallas kernels: 44.9 us -> 43.6 us
    pallas_call x1, Pallas kernels: 44.9 us -> 43.6 us  [per_device(): pl.pallas_call(kernel, out_shape=pltpu.VMEM((2, ROWS, 2048), F32), in_spe...]
where the time goes in v4:
time: 44.5 us; the launch traced here: 44.4 us
  Pallas kernels  43.6 us (98%)
  local copies, waits for them, and re-layouts  0.8 us (2%)
    pallas_call x1, Pallas kernels, per_device(): pl.pallas_call(kernel, out_shape=pltpu.VMEM((2, ROWS, 2048), F32), in_spe...  43.6 us

profile of v4, /device:TPU:1, one launch (start us, length us, event | category | flops | bytes accessed | tf_op | source)
XLA Modules:
  0.0 44.4 jit_solution(9966022499493761714)
XLA Ops:
  0.0 43.6 %shard_map.37 = f32[2,32,2048]{2,1,0:T(8,128)S(1)} custom-call(s32[32,512]{1,0:T(8,128)} %codes_in.1, s32[32,512]{1,0:T(8,128)} %aperture_in.1, s32[1,2]{1,0:T(1,128)} %bitcast.1), custom_call_target="tpu_custom_call" | custom-call | tf_op jit(solution)/shard_map/pallas_call | solution.py:415
  43.6 0.8 %copy.5 = f32[2,32,2048]{2,1,0:T(8,128)} copy(f32[2,32,2048]{2,1,0:T(8,128)S(1)} %shard_map.37) | data formatting | bytes 1048576

commit v5 on v4

--- a/solution.py
+++ b/solution.py
@@ -176,15 +176,14 @@
         p1r[g, own, :] = p1s[g, own, :]
 
     phase("tables")
-    shape = (512, 128)
+    shape = (256, 192)
     i, j = iota(shape, 0), iota(shape, 1)
-    source = j & 7
-    a = ((source >> 1) * NZ + ((j >> 3) & 7)) * NCORE + (source & 1)
-    cos, sin = cos_sin(a * (i & 255), 8)
-    w_high, w_low = halves(rotation(cos, sin, i >> 8, j >> 6))
-    wmat[:, 0:128] = w_high
-    wmat[:, 128:256] = w_high
-    wmat[:, 256:384] = w_low
+    for c in range(NCORE):
+        a = ((j & 3) * NZ + ((j >> 3) & 7)) * NCORE + c
+        cos, sin = cos_sin(a * (i & 127), 8)
+        weight = rotation(cos, sin, i >> 7, (j >> 2) & 1)
+        high = weight.astype(BF16).astype(F32)
+        wmat[c] = jnp.where(j < 128, high, weight - high).astype(BF16)
     shape = (256, 128)
     cos, sin = cos_sin((4 * iota(shape, 1) + x) * iota(shape, 0), 17)
     tcos[...] = cos
@@ -202,9 +201,11 @@
         messages = p1r.at[g, pl.ds(0, 56), :]
         remote(messages, messages, p1send, p1recv.at[g], at_z(right)).wait_recv()
         for n in range(GROWS):
-            for part in range(2):
-                gathered[z, g * GROWS + n, part * 8:(part + 1) * 8, :] = (
-                    p1r[g, pl.ds(part * GROWS + n, NB, stride=8), :])
+            for c in range(NCORE):
+                for part in range(2):
+                    spot = c * 8 + part * NX
+                    gathered[z, g * GROWS + n, spot:spot + NX, :] = (
+                        p1r[g, pl.ds(c * 8 + part * GROWS + n, NX, stride=8 * NCORE), :])
 
     def ring(block, group, way, step):
         part = gathered.at[block, pl.ds(group * GROWS, GROWS)]
@@ -242,7 +243,8 @@
 
     def small_y():
         remote(xslots.at[pl.ds(0, 7)], xslots.at[pl.ds(0, 7)], xsend, xrecv, at_z(right)).wait_recv()
-        yslots[y] = xslots[:, 0, :]
+        for k in range(NB):
+            yslots[y, k:k + 1, :] = xslots[k % NX * NCORE + k // NX, 0:1, :]
         @pl.when(y < NY - 1)
         def _():
             pl.semaphore_wait(ready_y, NY - 1 - y)
@@ -256,8 +258,10 @@
         def _(k):
             y_copy(k, k).wait_recv()
         before = lax.fori_loop(0, y, lambda k, acc: acc + yslots[k], jnp.zeros((NB, 128), F32))
-        zslots[z, 0:8, :] = before
-        zslots[z, 8:16, :] = xslots[:, 1, :]
+        shape = (NB, 128)
+        diagonal = jnp.where(iota(shape, 0) == (iota(shape, 1) & 7), before, 0.0)
+        zslots[z, 0:1, :] = jnp.sum(diagonal, axis=0, keepdims=True)
+        zslots[z, 1:2, :] = jnp.sum(xslots[:, 1, :], axis=0, keepdims=True)
         @pl.when(z < NZ - 2)
         def _():
             pl.semaphore_wait(ready_z, 5 + (z + 6) // 7 - z)
@@ -270,8 +274,18 @@
 
     def prefix():
         remote(zslots.at[pl.ds(0, 7)], zslots.at[pl.ds(0, 7)], azsend, azrecv, at_z(right)).wait_recv()
-        known.extend(cos_sin(zslots[:, 0:8, :].astype(I32), 12))
-        cslots[y] = jnp.sum(zslots[:, 8:16, :], axis=0)
+        shape = (NZ, 8, 128)
+        sublane, lane = iota(shape, 1), iota(shape, 2)
+        sign = jnp.where(sublane < NX, F32(-1.0), F32(1.0))
+        every = jnp.broadcast_to(zslots[:, 0:1, :], shape)
+        turns = []
+        for c in range(NCORE):
+            mine = jnp.where(lane == c * NX + (sublane & 3), every, 0.0)
+            before = jnp.broadcast_to(jnp.sum(mine, axis=2, keepdims=True), shape)
+            cos, sin = cos_sin(before.astype(I32), 12)
+            turns.append((cos, sin * sign))
+        known.append(turns)
+        cslots[y] = zslots[:, 1, :]
 
         @pl.loop(1, NY)
         def _(k):
@@ -290,43 +304,40 @@
                       asend, arecv.at[g], at_b(peer * NCORE + core))
 
     def transform(g):
-        pcos, psin = known[:2]
         for pair in range(GROWS // 2):
-            columns = []
-            for n in range(2):
-                block = gathered[:, g * GROWS + pair * 2 + n]
-                re, im = block[:, 0:8, :], block[:, 8:16, :]
-                columns.append(jnp.concatenate(
-                    [(re * pcos - im * psin).reshape(64, 128),
-                     (re * psin + im * pcos).reshape(64, 128)], axis=0))
-            high, low = halves(jnp.concatenate(columns, axis=1))
-            spec = jnp.dot(wmat[...], jnp.concatenate([high, low, high], axis=0),
-                           preferred_element_type=F32)
-            for n in range(2):
-                re = spec[0:256, n * 128:(n + 1) * 128]
-                im = spec[256:512, n * 128:(n + 1) * 128]
-                c, s = tcos[...], tsin[...]
-                turned = jnp.concatenate([re * c + im * s, im * c - re * s], axis=1)
-                high, low = halves(turned)
-                first = lax.dot_general(emat[...], high, nt, preferred_element_type=F32)
-                second = lax.dot_general(emat[0:32, :], low, nt, preferred_element_type=F32)
-                result = first[0:32] + first[32:64] + second
-                for h in range(2):
+            parity = []
+            for c in range(NCORE):
+                cos, sin = known[0][c]
+                columns = []
+                for n in range(2):
+                    block = gathered[:, g * GROWS + pair * 2 + n, c * 8:(c + 1) * 8, :]
+                    columns.append((block * cos + pltpu.roll(block, NX, axis=1) * sin).reshape(64, 128))
+                high, low = halves(jnp.concatenate(columns, axis=1))
+                parity.append(jnp.dot(wmat[c], jnp.concatenate([high, low, high], axis=0),
+                                      preferred_element_type=F32))
+            for h, spec in enumerate((parity[0] + parity[1], parity[0] - parity[1])):
+                c, s = tcos[h * 128:(h + 1) * 128, :], tsin[h * 128:(h + 1) * 128, :]
+                for n in range(2):
+                    re = spec[0:128, n * 128:(n + 1) * 128]
+                    im = spec[128:256, n * 128:(n + 1) * 128]
+                    turned = jnp.concatenate([re * c + im * s, im * c - re * s], axis=1)
+                    high, low = halves(turned)
+                    first = lax.dot_general(emat[...], high, nt, preferred_element_type=F32)
+                    second = lax.dot_general(emat[0:32, :], low, nt, preferred_element_type=F32)
                     zsend[g, h, pl.ds(pair * 2 + n, 32, stride=GROWS), :] = (
-                        result[:, h * 128:(h + 1) * 128])
-
-    def finish(g):
-        phase(f"fin{g}")
-        arrived((z + 4) % NZ, g)
-        if g == 0:
-            phase("azwait")
+                        first[0:32] + first[32:64] + second)
+
+    def finish(first, last):
+        if first == 0:
             prefix()
-        phase(f"dft{g}")
-        transform(g)
-        phase(f"asend{g}")
-        for k in (2, 1, 3):
-            a_copy(g, (x + k) % NX).start()
-        zrecv[x, g] = zsend[g, :, pl.ds(pl.multiple_of(x * 8 * GROWS, 8 * GROWS), 8 * GROWS), :]
+
+        @pl.loop(first, last)
+        def _(g):
+            arrived((z + 4) % NZ, g)
+            transform(g)
+            for k in (2, 1, 3):
+                a_copy(g, (x + k) % NX).start()
+            zrecv[x, g] = zsend[g, :, pl.ds(pl.multiple_of(x * 8 * GROWS, 8 * GROWS), 8 * GROWS), :]
 
     def b_copy(g, peer):
         return remote(fsend.at[g, peer],
@@ -334,10 +345,8 @@
                       bsend, brecv.at[g], at_b(peer))
 
     def combine(g):
-        phase(f"await{g}")
         remote(zrecv.at[pl.ds(0, 3), g], zrecv.at[pl.ds(0, 3), g], asend, arecv.at[g],
                at_z(right)).wait_recv()
-        phase(f"dft4_{g}")
         turn = jnp.where(iota((8, 128), 0) < GROWS, F32(1.0), F32(-1.0))
         for dc in range(2):
             for ql in range(2):
@@ -356,24 +365,28 @@
         landing[core, g, :, pl.ds(pl.multiple_of(x * 512, 512), 512)] = fsend[g, me]
 
     def deliver(g):
-        phase(f"bwait{g}")
-
         remote(fsend.at[g, pl.ds(0, 7)], fsend.at[g, pl.ds(0, 7)], bsend, brecv.at[g],
                at_z(right)).wait_recv()
-        if g == 0:
-            phase("cwait")
-            normalization()
-        phase(f"out{g}")
-        scale = known[2]
+        scale = known[1]
         for c in range(NCORE):
             for p in range(2):
-                out[p, c * HALF + g * GROWS:c * HALF + (g + 1) * GROWS, :] = (
+                out[p, pl.ds(c * HALF + g * GROWS, GROWS), :] = (
                     landing[c, g, p * GROWS:(p + 1) * GROWS, :] * scale)
 
-    for _, name, work in sorted(schedule(ring_step, finish, combine, deliver, small_y, small_z),
-                                key=lambda e: e[0]):
+    for _, name, work in sorted(schedule(ring_step, finish, small_y, small_z), key=lambda e: e[0]):
         phase(name)
         work()
+
+    phase("combine")
+    pl.loop(0, GROUPS)(combine)
+    phase("cwait")
+    normalization()
+    phase("deliver")
+    if LOOP_OUT:
+        pl.loop(0, GROUPS)(deliver)
+    else:
+        for g in range(GROUPS):
+            deliver(g)
 
     phase("drain")
 
@@ -389,24 +402,24 @@
     phase(None)
 
 
-def schedule(ring_step, finish, combine, deliver, small_y, small_z):
+def schedule(ring_step, finish, small_y, small_z):
     part = functools.partial
     events = [(SMALL[0], "ysmall", small_y), (SMALL[1], "zsmall", small_z)]
     for g in range(GROUPS):
         for step in range(4):
             events.append((RING[step] + g * LAG, f"r{step}{g}", part(ring_step, step, g)))
-    for g in range(GROUPS):
-        events.append((FIN[g], f"fin{g}", part(finish, g)))
-        events.append((FOUR[g], f"await{g}", part(combine, g)))
-        events.append((100.0 + g, f"bwait{g}", part(deliver, g)))
+    for k in range(len(FIN)):
+        first, when = FIN[k]
+        last = FIN[k + 1][0] if k + 1 < len(FIN) else GROUPS
+        events.append((when, f"fin{first}", part(finish, first, last)))
     return events
 
 
 RING = (0.0, 2.2, 4.4, 6.6)
 LAG = 1.0
 SMALL = (2.3, 6.0)
-FIN = (8.8, 10.0, 11.2, 12.4)
-FOUR = (13.5, 15.0, 16.5, 18.0)
+FIN = ((0, 8.8), (1, 10.0))
+LOOP_OUT = False
 
 
 def per_device(phase_codes, aperture, tile_offsets):
@@ -419,11 +432,11 @@
         out_specs=pl.BlockSpec(memory_space=pltpu.VMEM),
         scratch_shapes=[
             vmem((ROWS, 512), I32), vmem((ROWS, 512), I32), vmem((1, 2), I32),
-            vmem((NB, 2, 128), F32), vmem((NY, NB, 128), F32), vmem((NZ, 16, 128), F32), vmem((NY, NB, 128), F32),
+            vmem((NB, 2, 128), F32), vmem((NY, NB, 128), F32), vmem((NZ, 2, 128), F32), vmem((NY, NB, 128), F32),
             vmem((GROUPS, NB * 8, 128), F32), vmem((GROUPS, NB * 8, 128), F32),
             vmem((NZ, HALF, 16, 128), F32),
             vmem((256, 128), F32), vmem((256, 128), F32),
-            vmem((512, 384), BF16), vmem((64, 256), BF16),
+            vmem((NCORE, 256, 192), BF16), vmem((64, 256), BF16),
             vmem((GROUPS, 2, 32 * GROWS, 128), F32),
             vmem((NX, GROUPS, 2, 8 * GROWS, 128), F32),
             vmem((GROUPS, NB, 2 * GROWS, 512), F32),

time: 44.5 us -> 44 us (0.989)
  Pallas kernels: 43.6 us -> 42.9 us
    pallas_call x1, Pallas kernels: 43.6 us -> 42.9 us  [per_device(): pl.pallas_call(kernel, out_shape=pltpu.VMEM((2, ROWS, 2048), F32), in_spe...]
where the time goes in v5:
time: 44 us; the launch traced here: 43.7 us
  Pallas kernels  42.9 us (98%)
  local copies, waits for them, and re-layouts  0.8 us (2%)
    pallas_call x1, Pallas kernels, per_device(): pl.pallas_call(kernel, out_shape=pltpu.VMEM((2, ROWS, 2048), F32), in_spe...  42.9 us

profile of v5, /device:TPU:1, one launch (start us, length us, event | category | flops | bytes accessed | tf_op | source)
XLA Modules:
  0.0 43.7 jit_solution(7766797672037067251)
XLA Ops:
  0.0 42.9 %shard_map.37 = f32[2,32,2048]{2,1,0:T(8,128)S(1)} custom-call(s32[32,512]{1,0:T(8,128)} %codes_in.1, s32[32,512]{1,0:T(8,128)} %aperture_in.1, s32[1,2]{1,0:T(1,128)} %bitcast.1), custom_call_target="tpu_custom_call" | custom-call | tf_op jit(solution)/shard_map/pallas_call | solution.py:428
  42.9 0.8 %copy.5 = f32[2,32,2048]{2,1,0:T(8,128)} copy(f32[2,32,2048]{2,1,0:T(8,128)S(1)} %shard_map.37) | data formatting | bytes 1048576

commit v6 on v5

--- a/solution.py
+++ b/solution.py
@@ -56,7 +56,7 @@
 
 
 def kernel(codes_in, aperture_in, offsets_in, out, codes, aperture, offsets, xslots, yslots, zslots, cslots,
-           p1s, p1r, gathered, tcos, tsin, wmat, emat, zsend, zrecv, fsend, landing,
+           p1s, p1r, gathered, tcos, tsin, wmat, emat, zsend, zrecv, fsend, landing, turns,
            ready_y, ready_z, insem, p1send, p1recv, xsend, xrecv, ysend, yrecv, azsend, azrecv, csend, crecv,
            p2send, p2recv, asend, arecv, bsend, brecv):
     y = lax.axis_index("row")
@@ -278,13 +278,12 @@
         sublane, lane = iota(shape, 1), iota(shape, 2)
         sign = jnp.where(sublane < NX, F32(-1.0), F32(1.0))
         every = jnp.broadcast_to(zslots[:, 0:1, :], shape)
-        turns = []
         for c in range(NCORE):
             mine = jnp.where(lane == c * NX + (sublane & 3), every, 0.0)
             before = jnp.broadcast_to(jnp.sum(mine, axis=2, keepdims=True), shape)
             cos, sin = cos_sin(before.astype(I32), 12)
-            turns.append((cos, sin * sign))
-        known.append(turns)
+            turns[c, 0] = cos
+            turns[c, 1] = sin * sign
         cslots[y] = zslots[:, 1, :]
 
         @pl.loop(1, NY)
@@ -307,11 +306,11 @@
         for pair in range(GROWS // 2):
             parity = []
             for c in range(NCORE):
-                cos, sin = known[0][c]
                 columns = []
                 for n in range(2):
                     block = gathered[:, g * GROWS + pair * 2 + n, c * 8:(c + 1) * 8, :]
-                    columns.append((block * cos + pltpu.roll(block, NX, axis=1) * sin).reshape(64, 128))
+                    turned = block * turns[c, 0] + pltpu.roll(block, NX, axis=1) * turns[c, 1]
+                    columns.append(turned.reshape(64, 128))
                 high, low = halves(jnp.concatenate(columns, axis=1))
                 parity.append(jnp.dot(wmat[c], jnp.concatenate([high, low, high], axis=0),
                                       preferred_element_type=F32))
@@ -367,7 +366,7 @@
     def deliver(g):
         remote(fsend.at[g, pl.ds(0, 7)], fsend.at[g, pl.ds(0, 7)], bsend, brecv.at[g],
                at_z(right)).wait_recv()
-        scale = known[1]
+        scale = known[0]
         for c in range(NCORE):
             for p in range(2):
                 out[p, pl.ds(c * HALF + g * GROWS, GROWS), :] = (
@@ -441,6 +440,7 @@
             vmem((NX, GROUPS, 2, 8 * GROWS, 128), F32),
             vmem((GROUPS, NB, 2 * GROWS, 512), F32),
             vmem((NCORE, GROUPS, 2 * GROWS, 2048), F32),
+            vmem((NCORE, 2, NZ, 8, 128), F32),
             pltpu.SemaphoreType.REGULAR, pltpu.SemaphoreType.REGULAR, dma((3,)),
             dma, dma((GROUPS,)), dma, dma, dma((NY,)), dma((NY,)), dma, dma, dma, dma,
             dma, dma((NZ, GROUPS)), dma, dma((GROUPS,)), dma, dma((GROUPS,)),

time: 44 us -> 44 us (level)
  no operation moved by 1% of the time
where the time goes in v6:
time: 44 us; the launch traced here: 43.7 us
  Pallas kernels  42.9 us (98%)
  local copies, waits for them, and re-layouts  0.8 us (2%)
    pallas_call x1, Pallas kernels, per_device(): pl.pallas_call(kernel, out_shape=pltpu.VMEM((2, ROWS, 2048), F32), in_spe...  42.9 us

profile of v6, /device:TPU:1, one launch (start us, length us, event | category | flops | bytes accessed | tf_op | source)
XLA Modules:
  0.0 43.7 jit_solution(7089422047393268615)
XLA Ops:
  0.0 42.9 %shard_map.37 = f32[2,32,2048]{2,1,0:T(8,128)S(1)} custom-call(s32[32,512]{1,0:T(8,128)} %codes_in.1, s32[32,512]{1,0:T(8,128)} %aperture_in.1, s32[1,2]{1,0:T(1,128)} %bitcast.1), custom_call_target="tpu_custom_call" | custom-call | tf_op jit(solution)/shard_map/pallas_call | solution.py:427
  42.9 0.8 %copy.5 = f32[2,32,2048]{2,1,0:T(8,128)} copy(f32[2,32,2048]{2,1,0:T(8,128)S(1)} %shard_map.37) | data formatting | bytes 1048576

commit v7 on v5

--- a/solution.py
+++ b/solution.py
@@ -417,7 +417,7 @@
 
 RING = (0.0, 2.2, 4.4, 6.6)
 LAG = 1.0
-SMALL = (2.3, 6.0)
+SMALL = (2.3, 5.3)
 FIN = ((0, 8.8), (1, 10.0))
 LOOP_OUT = False
 

time: 44 us -> 43.9 us (level)
  no operation moved by 1% of the time
where the time goes in v7:
time: 43.9 us; the launch traced here: 43.6 us
  Pallas kernels  42.8 us (97%)
  local copies, waits for them, and re-layouts  0.8 us (2%)
    pallas_call x1, Pallas kernels, per_device(): pl.pallas_call(kernel, out_shape=pltpu.VMEM((2, ROWS, 2048), F32), in_spe...  42.8 us

profile of v7, /device:TPU:1, one launch (start us, length us, event | category | flops | bytes accessed | tf_op | source)
XLA Modules:
  0.0 43.6 jit_solution(5976193907905079266)
XLA Ops:
  0.0 42.8 %shard_map.37 = f32[2,32,2048]{2,1,0:T(8,128)S(1)} custom-call(s32[32,512]{1,0:T(8,128)} %codes_in.1, s32[32,512]{1,0:T(8,128)} %aperture_in.1, s32[1,2]{1,0:T(1,128)} %bitcast.1), custom_call_target="tpu_custom_call" | custom-call | tf_op jit(solution)/shard_map/pallas_call | solution.py:428
  42.8 0.8 %copy.5 = f32[2,32,2048]{2,1,0:T(8,128)} copy(f32[2,32,2048]{2,1,0:T(8,128)S(1)} %shard_map.37) | data formatting | bytes 1048576
